TPU v7x, 256 devices: a whole 4x4x8 slice. The times are simulated.
256 devices in a mesh: clip: 128 (over z, y, x), mp: 2 (over core).
Axes of the slice: x: 4, y: 4, z: 8, core: 2. Of those that a mesh axis runs over, the one named last changes fastest.
Arguments:
- tokens: bfloat16 [384, 128, 1024], P('clip', None, 'mp'), may hold values from -6 to 6
- bottleneck: bfloat16 [128, 4, 1024], P('clip', None, 'mp'), may hold values from -6 to 6
- clip_lengths: int32 [128], replicated, may hold values from 2 to 4, as said below
- video_blocks: int32 [128], replicated, may hold values from 1 to 3, as said below
- store_map: int32 [128, 3], replicated, may hold values from -1 to 511, as said below
- norm1_gain: float32 [1024], replicated, may hold values from 0.4 to 1.6
- w_qkv: bfloat16 [3, 1024, 1024], P(None, None, 'mp'), may hold values from -0.625 to 0.625
- w_out: bfloat16 [1024, 1024], P('mp'), may hold values from -0.1875 to 0.1875
- norm2_gain: float32 [1024], replicated, may hold values from 0.4 to 1.6
- w_up: bfloat16 [1024, 4096], P(None, 'mp'), may hold values from -0.1875 to 0.1875
- w_down: bfloat16 [4096, 1024], P('mp'), may hold values from -0.09375 to 0.09375
Outputs:
- mixed_tokens: bfloat16 [384, 128, 1024], P('clip', None, 'mp')
- merged_bottleneck: bfloat16 [128, 4, 1024], P('clip', None, 'mp')
Inputs may be any that keep to these rules, and one draw needn't show every extreme that they name: clip_lengths[c] counts the blocks of the clip owned by index c of clip. The first video_blocks[c] blocks of clip c are video, the others up to clip_lengths[c] audio; video_blocks[c] <= clip_lengths[c] - 1. store_map[d, s] = c * 4 + b when slot s of device d along clip holds block b of clip c, and -1 when the slot is empty; each block b < clip_lengths[c] of each clip sits in exactly one slot, on a device of the same aligned group of 4 devices along clip as c; no device holds two blocks of one clip.
All inputs are finite; a program needn't handle non-finite values.
Results may differ from a plain program's by a relative error of at most 0.006.
Values may be sent and summed in bfloat16 or wider, within the bound.
No kernel may reach another device: no remote copies, remote signals or barrier semaphores. Data moves between devices by JAX's collectives and lax.ppermute only.
A program may use at most 128 MiB of HBM per device.

v0:
```python
import jax
import jax.numpy as jnp
from jax import lax
from jax.experimental import pallas as pl
from jax.experimental.pallas import tpu as pltpu
from jax.sharding import PartitionSpec as P

HEAD_DIM = 64
BLK = 128
NB = 4
SLOT_DEV = 4
STORE_DEV = 3
GROUP = 4
PAD = 16
STORED = STORE_DEV * BLK
ROWS = STORED + PAD
CLIP_ROWS = SLOT_DEV * BLK
STEPS = (2, 1, 3)
BF16 = jnp.bfloat16
F32 = jnp.float32

VMEM = pl.BlockSpec(memory_space=pltpu.VMEM)
HBM = pl.BlockSpec(memory_space=pltpu.HBM)
DMA = pltpu.SemaphoreType.DMA
SMEM = pl.BlockSpec(memory_space=pltpu.SMEM)


def spec(shape, dtype=BF16):
    return jax.ShapeDtypeStruct(shape, dtype)


def partner(x, step):
    return lax.ppermute(x, "clip", [(i, i ^ step) for i in range(lax.axis_size("clip"))])


def slot_for(store_map, device, owner):
    slot = jnp.int32(-1)
    block = jnp.int32(-1)
    for s in range(STORE_DEV):
        entry = store_map[s, device]
        hit = (entry >= 0) & (entry // SLOT_DEV == owner)
        slot = jnp.where(hit, s, slot)
        block = jnp.where(hit, entry % SLOT_DEV, block)
    return slot, block


def norm_into(x0, x1, gain, out, at, rows):
    half = x0.shape[1]
    x0 = x0.astype(F32)
    x1 = x1.astype(F32)
    scale = 1.0 / (2 * half)
    mean = (jnp.sum(x0, axis=-1, keepdims=True) + jnp.sum(x1, axis=-1, keepdims=True)) * scale
    x0 = x0 - mean
    x1 = x1 - mean
    moment = (
        jnp.sum(x0 * x0, axis=-1, keepdims=True) + jnp.sum(x1 * x1, axis=-1, keepdims=True)
    ) * scale
    inv = lax.rsqrt(moment + 1e-05)
    out[pl.ds(at, rows), :half] = (x0 * inv * gain[:, :half]).astype(BF16)
    out[pl.ds(at, rows), half:] = (x1 * inv * gain[:, half:]).astype(BF16)


def pack_kernel(slots, tokens, extra, far, near, across, stored, store_map, blocks, few, sems):
    member = lax.axis_index("clip")
    loads = [
        pltpu.make_async_copy(x, y, sems.at[i])
        for i, (x, y) in enumerate(((slots, store_map), (tokens, blocks), (extra, few)))
    ]
    for load in loads:
        load.start()
    for load in loads:
        load.wait()
    for step, out in zip(STEPS, (far, near, across)):
        slot, _ = slot_for(store_map, member, member ^ step)
        out[...] = blocks[jnp.maximum(slot, 0)]
    for s in range(STORE_DEV):
        stored[s * BLK : (s + 1) * BLK, :] = blocks[s]
    width = stored.shape[1]
    stored[STORED:, :] = jnp.concatenate(
        [few[0].astype(F32), jnp.zeros((PAD - NB, width), F32)], axis=0
    ).astype(BF16)


def ready_kernel(
    slots,
    all_lengths,
    all_videos,
    gain_in,
    w_qkv,
    stored,
    weights,
    query,
    keys,
    values,
    gain,
    facts,
    normed,
    info,
    store_map,
    lengths,
    videos,
    sems,
):
    member = lax.axis_index("clip")
    small = [
        pltpu.make_async_copy(x, y, sems.at[i])
        for i, (x, y) in enumerate(
            ((gain_in, gain), (slots, store_map), (all_lengths, lengths), (all_videos, videos))
        )
    ]
    loads = [pltpu.make_async_copy(w_qkv.at[i], weights.at[i], sems.at[5 + i]) for i in range(3)]
    for load in small + loads:
        load.start()
    small[0].wait()
    gains = gain[...]
    norm_into(stored[0, STORED:, :], stored[1, STORED:, :], gains, normed, BLK, PAD)
    for load in small[1:]:
        load.wait()
    slot, block = slot_for(store_map, member, member)
    for place, step in enumerate(STEPS):
        info[0, place] = slot_for(store_map, member ^ step, member)[1]
    info[0, GROUP - 1] = block
    info[0, GROUP] = lengths[member]
    info[0, GROUP + 1] = videos[member]
    keep = pltpu.make_async_copy(info, facts, sems.at[4])
    keep.start()
    here = pl.multiple_of(jnp.maximum(slot, 0) * BLK, BLK)
    norm_into(
        stored[0, pl.ds(here, BLK), :], stored[1, pl.ds(here, BLK), :], gains, normed, 0, BLK
    )
    width = query.shape[1]
    tile = 256
    for which, out in ((0, query), (1, keys)):
        loads[which].wait()
        for j in range(0, width, tile):
            got = jnp.dot(normed[...], weights[which, :, j : j + tile], preferred_element_type=F32)
            if which == 0:
                got = got * HEAD_DIM ** (-0.5)
            out[:, j : j + tile] = got.astype(BF16)
    loads[2].wait()
    for j in range(0, width, tile):
        got = jnp.dot(normed[...], weights[2, :, j : j + tile], preferred_element_type=F32)
        for k in range(tile // BLK):
            p = j // BLK + k
            cols = slice(k * BLK, (k + 1) * BLK)
            values[p, :, :BLK] = got[:BLK, cols].T.astype(BF16)
            values[p, :, BLK:] = got[BLK:, cols].T.astype(BF16)
    keep.wait()


NT = (((1,), (1,)), ((), ()))
END = CLIP_ROWS + PAD


def token_block(query, keys, values, context, place, block, first, count):
    pairs = values.shape[0]
    low = lax.broadcasted_iota(jnp.int32, (BLK, BLK), 1) < HEAD_DIM
    real = lax.broadcasted_iota(jnp.int32, (PAD, 2 * BLK), 0) < NB
    start = pl.multiple_of(first * BLK, BLK)
    at = pl.multiple_of(block * BLK, BLK)
    seen = count * BLK
    cols = [slice(p * BLK, (p + 1) * BLK) for p in range(pairs)]
    scores = []
    for p in range(pairs):
        q = query[pl.ds(at, BLK), cols[p]]
        none = jnp.zeros_like(q)
        both = jnp.concatenate([jnp.where(low, q, none), jnp.where(low, none, q)], axis=0)
        k = jnp.concatenate([keys[pl.ds(start, seen), cols[p]], keys[CLIP_ROWS:END, cols[p]]], axis=0)
        s = lax.dot_general(k, both, NT, preferred_element_type=F32)
        scores.append((s[:seen], jnp.where(real, s[seen:], -1e30)))
    tops = [
        jnp.maximum(jnp.max(s, axis=0, keepdims=True), jnp.max(se, axis=0, keepdims=True))
        for s, se in scores
    ]
    parts = [
        jnp.concatenate([jnp.exp(s - top).astype(BF16), jnp.exp(se - top).astype(BF16)], axis=0)
        for (s, se), top in zip(scores, tops)
    ]
    sums = []
    for p in range(pairs):
        v = jnp.concatenate([values[p, :, pl.ds(start, seen)], values[p, :, CLIP_ROWS:END]], axis=1)
        sums.append(jnp.dot(v, parts[p], preferred_element_type=F32))
    for p in range(pairs):
        o = sums[p]
        total = o[BLK : BLK + 1]
        o = jnp.concatenate(
            [o[:HEAD_DIM, :BLK] / total[:, :BLK], o[HEAD_DIM:BLK, BLK:] / total[:, BLK:]], axis=0
        )
        context[place, :, cols[p]] = o.T.astype(BF16)


def visit_blocks(info, places, query, keys, values, context):
    def visit(i, carry):
        place = places[0] + i * (places[1] - places[0])
        block = info[0, place]
        length = info[0, GROUP]
        video = info[0, GROUP + 1]
        is_video = block < video
        first = jnp.where(is_video, 0, video)
        seen = jnp.where(is_video, video, length - video)
        for count in range(1, SLOT_DEV):

            @pl.when((block >= 0) & (seen == count))
            def _():
                token_block(query, keys, values, context, i, block, first, count)

        return carry

    lax.fori_loop(0, 2, visit, 0)


def attend_kernel(
    facts,
    gain,
    arrived,
    weights,
    own_query,
    own_keys,
    own_values,
    far,
    across,
    query,
    keys,
    values,
    normed,
    context,
    info,
    sems,
):
    load = pltpu.make_async_copy(facts, info, sems.at[0])
    load.start()
    width = query.shape[1]
    pairs = width // BLK
    context[...] = jnp.zeros_like(context)
    gains = gain[...]
    for k in range(GROUP - 1):
        rows = slice(k * BLK, (k + 1) * BLK)
        norm_into(arrived[0, rows, :], arrived[1, rows, :], gains, normed, k * BLK, BLK)
    load.wait()
    length = info[0, GROUP]
    row_at = []
    for place in range(GROUP):
        block = info[0, place]
        row_at.append(pl.multiple_of(jnp.where(block < 0, SLOT_DEV + 1, block) * BLK, BLK))

    last = GROUP - 1
    for own, out in ((own_query, query), (own_keys, keys)):
        out[pl.ds(row_at[last], BLK), :] = own[:BLK, :]
        out[CLIP_ROWS:END, :] = own[BLK:, :]
    for p in range(pairs):
        values[p, :BLK, pl.ds(row_at[last], BLK)] = own_values[p, :, :BLK]
        values[p, :BLK, CLIP_ROWS:END] = own_values[p, :, BLK:]
        values[p, BLK:, :END] = jnp.ones((PAD, END), BF16)
    tile = 256
    for which, out in ((0, query), (1, keys)):
        for j in range(0, width, tile):
            got = jnp.dot(normed[...], weights[which, :, j : j + tile], preferred_element_type=F32)
            if which == 0:
                got = got * HEAD_DIM ** (-0.5)
            got = got.astype(BF16)
            for place in range(last):
                out[pl.ds(row_at[place], BLK), j : j + tile] = got[place * BLK : (place + 1) * BLK]
    for j in range(0, width, tile):
        got = jnp.dot(normed[...], weights[2, :, j : j + tile], preferred_element_type=F32)
        for k in range(tile // BLK):
            p = j // BLK + k
            cols = slice(k * BLK, (k + 1) * BLK)
            for place in range(last):
                turned = got[place * BLK : (place + 1) * BLK, cols].T
                values[p, :BLK, pl.ds(row_at[place], BLK)] = turned.astype(BF16)
    for b in range(2, SLOT_DEV):

        @pl.when(b >= length)
        def _():
            values[:, :BLK, b * BLK : (b + 1) * BLK] = jnp.zeros((pairs, BLK, BLK), BF16)

    visit_blocks(info, (0, 2), query, keys, values, context)
    far[...] = context[0]
    across[...] = context[1]


def rest_kernel(query, keys, values, facts, near, own, context, info, sems):
    load = pltpu.make_async_copy(facts, info, sems.at[0])
    load.start()
    width = query.shape[1]
    pairs = width // BLK
    context[...] = jnp.zeros_like(context)
    load.wait()
    length = info[0, GROUP]
    video = info[0, GROUP + 1]
    visit_blocks(info, (1, 3), query, keys, values, context)
    near[...] = context[0]
    own[:BLK, :] = context[1]

    heads = width // HEAD_DIM
    sub = 8
    qe = query[CLIP_ROWS:END, :].astype(F32)[:sub]
    qe = jnp.concatenate([qe] * heads, axis=0)
    row_head = lax.broadcasted_iota(jnp.int32, (heads * sub, width), 0) // sub
    col_head = lax.broadcasted_iota(jnp.int32, (heads * sub, width), 1) // HEAD_DIM
    qe = jnp.where(row_head == col_head, qe, 0.0).astype(BF16)
    s = lax.dot_general(qe, keys[:END, :], NT, preferred_element_type=F32)
    col = lax.broadcasted_iota(jnp.int32, s.shape, 1)
    bottle = (col >= CLIP_ROWS) & (col < CLIP_ROWS + NB)
    parts = []
    for allowed in (
        bottle | (col < video * BLK),
        bottle | ((col >= video * BLK) & (col < length * BLK)),
    ):
        masked = jnp.where(allowed, s, -1e30)
        e = jnp.exp(masked - jnp.max(masked, axis=-1, keepdims=True))
        parts.append((e / jnp.sum(e, axis=-1, keepdims=True)).astype(BF16))
    first_head = lax.broadcasted_iota(jnp.int32, (sub, BLK), 1) < HEAD_DIM
    for p in range(pairs):
        rows = slice(2 * p * sub, (2 * p + 2) * sub)
        both = jnp.concatenate([parts[0][rows], parts[1][rows]], axis=0)
        o = lax.dot_general(both, values[p, :BLK, :END], NT, preferred_element_type=F32)
        o = 0.5 * (o[: 2 * sub] + o[2 * sub :])
        o = jnp.where(first_head, o[:sub], o[sub:])
        own[BLK:, p * BLK : (p + 1) * BLK] = jnp.concatenate([o, jnp.zeros_like(o)], axis=0).astype(BF16)


def feed_kernel(
    store_map,
    stored,
    own,
    arrived,
    w_out,
    w_out_other,
    gain,
    w_up,
    w_down,
    base,
    send,
    context,
    after,
    normed,
    active,
):
    member = lax.axis_index("clip")
    core = lax.axis_index("mp")
    half = base.shape[1]
    hidden = w_up.shape[1]
    sides = (core, 1 - core)
    kept = [
        (slice(s * BLK, (s + 1) * BLK), store_map[s, member] >= 0) for s in range(STORE_DEV)
    ] + [(slice(STORED, ROWS), True)]
    for s in range(STORE_DEV):
        entry = store_map[s, member]
        step = jnp.where(entry >= 0, (entry // SLOT_DEV) ^ member, -1)
        at = jnp.where(step == STEPS[0], 0, jnp.where(step == STEPS[1], 1, 2))
        at = pl.multiple_of(at * BLK, BLK)
        rows = slice(s * BLK, (s + 1) * BLK)

        @pl.when(step == 0)
        def _():
            for k in range(2):
                context[k, rows, :] = own[sides[k], :BLK, :]

        @pl.when(step > 0)
        def _():
            for k in range(2):
                context[k, rows, :] = arrived[sides[k], pl.ds(at, BLK), :]

        @pl.when(step < 0)
        def _():
            for k in range(2):
                context[k, rows, :] = jnp.zeros((BLK, half), BF16)

    for k in range(2):
        context[k, STORED:, :] = own[sides[k], BLK:, :]

    tile = 256
    for j in range(0, 2 * half, tile):
        got = jnp.dot(context[0], w_out[:, j : j + tile], preferred_element_type=F32)
        got = got + jnp.dot(context[1], w_out_other[:, j : j + tile], preferred_element_type=F32)
        side, off = divmod(j, half)
        got = got + stored[side, :, off : off + tile].astype(F32)
        after[:, j : j + tile] = got.astype(BF16)
    gains = gain[...]
    for r in range(0, ROWS, 80):
        norm_into(after[r : r + 80, :half], after[r : r + 80, half:], gains, normed, r, 80)
    for j in range(0, hidden, tile):
        got = jnp.dot(normed[...], w_up[:, j : j + tile], preferred_element_type=F32)
        active[:, j : j + tile] = jax.nn.gelu(got, approximate=True).astype(BF16)
    for j in range(0, half, tile):
        other = pl.multiple_of((1 - core) * half + j, tile)
        got = jnp.dot(active[...], w_down[:, pl.ds(other, tile)], preferred_element_type=F32)
        for rows, keep in kept:
            send[rows, j : j + tile] = jnp.where(keep, got[rows], 0.0).astype(BF16)
        mine = pl.multiple_of(core * half + j, tile)
        got = jnp.dot(active[...], w_down[:, pl.ds(mine, tile)], preferred_element_type=F32)
        got = got + after[:, pl.ds(mine, tile)].astype(F32)
        for rows, keep in kept:
            base[rows, j : j + tile] = jnp.where(keep, got[rows], 0.0)


def finish_kernel(base, sums, mixed, merged):
    other = 1 - lax.axis_index("mp")
    for s in range(STORE_DEV):
        rows = slice(s * BLK, (s + 1) * BLK)
        mixed[s] = (base[rows, :] + sums[other, rows, :].astype(F32)).astype(BF16)
    got = base[STORED:, :] + sums[other, STORED:, :].astype(F32)
    merged[0] = got[:NB].astype(BF16)


def stay(x):
    return pltpu.with_memory_space_constraint(x, pltpu.HBM)


def ready(slots, clip_lengths, video_blocks, gain1, w_qkv, stored_all):
    model = w_qkv.shape[1]
    width = w_qkv.shape[2]
    pairs = width // BLK
    info = (1, 2 * GROUP)
    return pl.pallas_call(
        ready_kernel,
        name="ready",
        out_shape=(
            spec(w_qkv.shape),
            spec((BLK + PAD, width)),
            spec((BLK + PAD, width)),
            spec((pairs, BLK, BLK + PAD)),
            spec((1, model), F32),
            spec(info, jnp.int32),
        ),
        in_specs=[HBM] * 5 + [VMEM],
        out_specs=(VMEM,) * 6,
        scratch_shapes=[
            pltpu.VMEM((BLK + PAD, model), BF16),
            pltpu.SMEM(info, jnp.int32),
            pltpu.SMEM(slots.shape, jnp.int32),
            pltpu.SMEM(clip_lengths.shape, jnp.int32),
            pltpu.SMEM(video_blocks.shape, jnp.int32),
            DMA((8,)),
        ],
        compiler_params=pltpu.CompilerParams(vmem_limit_bytes=8 << 20),
        cost_estimate=pl.CostEstimate(flops=450000000, bytes_accessed=4000000, transcendentals=0),
    )(stay(slots), stay(clip_lengths), stay(video_blocks), stay(gain1), stay(w_qkv), stored_all)


def attend(facts, gain, arrived, weights, own_qkv):
    model = weights.shape[1]
    width = weights.shape[2]
    pairs = width // BLK
    rows = CLIP_ROWS + 2 * BLK
    block = spec((BLK, width))
    return pl.pallas_call(
        attend_kernel,
        name="attend",
        out_shape=(
            block,
            block,
            spec((rows, width)),
            spec((rows, width)),
            spec((pairs, BLK + PAD, rows)),
        ),
        in_specs=[VMEM] * 7,
        out_specs=(VMEM,) * 5,
        scratch_shapes=[
            pltpu.VMEM(((GROUP - 1) * BLK, model), BF16),
            pltpu.VMEM((2, BLK, width), BF16),
            pltpu.SMEM(facts.shape, jnp.int32),
            DMA((1,)),
        ],
        compiler_params=pltpu.CompilerParams(vmem_limit_bytes=16 << 20),
        cost_estimate=pl.CostEstimate(flops=1800000000, bytes_accessed=6000000, transcendentals=1500000),
    )(facts, gain, arrived, weights, *own_qkv)


def rest(query, keys, values, facts):
    width = query.shape[1]
    info = (1, 2 * GROUP)
    return pl.pallas_call(
        rest_kernel,
        name="rest",
        out_shape=(spec((BLK, width)), spec((BLK + PAD, width))),
        in_specs=[VMEM] * 4,
        out_specs=(VMEM,) * 2,
        scratch_shapes=[
            pltpu.VMEM((2, BLK, width), BF16),
            pltpu.SMEM(info, jnp.int32),
            DMA((1,)),
        ],
        compiler_params=pltpu.CompilerParams(vmem_limit_bytes=16 << 20),
        cost_estimate=pl.CostEstimate(flops=700000000, bytes_accessed=3000000, transcendentals=1500000),
    )(query, keys, values, facts)


def feed(slots, stored_all, own_all, arrived, w_out, w_out_other, gain2, w_up, w_down):
    width = stored_all.shape[2]
    model = 2 * width
    hidden = w_up.shape[1]
    return pl.pallas_call(
        feed_kernel,
        name="feed",
        out_shape=(spec((ROWS, width), F32), spec((ROWS, width))),
        in_specs=[SMEM] + [VMEM] * 8,
        out_specs=(VMEM,) * 2,
        scratch_shapes=[
            pltpu.VMEM((2, ROWS, width), BF16),
            pltpu.VMEM((ROWS, model), BF16),
            pltpu.VMEM((ROWS, model), BF16),
            pltpu.VMEM((ROWS, hidden), BF16),
        ],
        compiler_params=pltpu.CompilerParams(vmem_limit_bytes=16 << 20),
        cost_estimate=pl.CostEstimate(flops=4100000000, bytes_accessed=14000000, transcendentals=820000),
    )(slots, stored_all, own_all, arrived, w_out, w_out_other, gain2, w_up, w_down)


def body(
    tokens,
    bottleneck,
    clip_lengths,
    video_blocks,
    store_map,
    norm1_gain,
    w_qkv,
    w_out,
    norm2_gain,
    w_up,
    w_down,
):
    width = tokens.shape[2]
    model = 2 * width
    gain1 = norm1_gain.reshape(1, model)
    gain2 = norm2_gain.reshape(1, model)
    block = spec((BLK, width))
    slots = store_map.T

    far, near, across, stored = pl.pallas_call(
        pack_kernel,
        name="pack",
        out_shape=(block, block, block, spec((ROWS, width))),
        in_specs=[HBM, HBM, HBM],
        out_specs=(VMEM,) * 4,
        scratch_shapes=[
            pltpu.SMEM(slots.shape, jnp.int32),
            pltpu.VMEM(tokens.shape, BF16),
            pltpu.VMEM(bottleneck.shape, BF16),
            DMA((3,)),
        ],
        compiler_params=pltpu.CompilerParams(vmem_limit_bytes=4 << 20),
    )(stay(slots), stay(tokens), stay(bottleneck))
    far = partner(far, 2)
    near = partner(near, 1)
    across = partner(across, 3)
    stored_all = lax.all_gather(stored, "mp", axis=0)
    stored_all, w_out_late = lax.optimization_barrier((stored_all, w_out))
    w_out_other = lax.ppermute(w_out_late, "mp", [(0, 1), (1, 0)])
    weights, *own_qkv, gain, facts = ready(
        slots, clip_lengths, video_blocks, gain1, w_qkv, stored_all
    )
    arrived = lax.all_gather(jnp.concatenate([far, near, across], axis=0), "mp", axis=0)

    far, across, query, keys, values = attend(facts, gain, arrived, weights, own_qkv)
    far = partner(far, 2)
    across = partner(across, 3)
    near, own = rest(query, keys, values, facts)
    near = partner(near, 1)
    own, far = lax.optimization_barrier((own, far))
    own_all = lax.all_gather(own, "mp", axis=0)
    arrived = lax.all_gather(jnp.concatenate([far, near, across], axis=0), "mp", axis=0)

    base, send = feed(
        slots, stored_all, own_all, arrived, w_out, w_out_other, gain2, w_up, w_down
    )
    sums = lax.all_gather(send, "mp", axis=0)

    mixed, merged = pl.pallas_call(
        finish_kernel,
        name="finish",
        out_shape=(spec(tokens.shape), spec(bottleneck.shape)),
        in_specs=[VMEM, VMEM],
        out_specs=(VMEM,) * 2,
        compiler_params=pltpu.CompilerParams(vmem_limit_bytes=8 << 20),
    )(base, sums)
    return mixed, merged


def solution(mesh):
    placed = (
        P("clip", None, "mp"),
        P("clip", None, "mp"),
        P(),
        P(),
        P(),
        P(),
        P(None, None, "mp"),
        P("mp", None),
        P(),
        P(None, "mp"),
        P("mp", None),
    )
    return jax.shard_map(
        body,
        mesh=mesh,
        in_specs=placed,
        out_specs=(P("clip", None, "mp"), P("clip", None, "mp")),
        check_vma=False,
    )
```

profile of v0, /device:TPU:1, one launch (start us, length us, event | category | flops | bytes accessed | tf_op | source)
XLA Modules:
  0.0 42.5 jit_solution(7489484287815154992)
XLA Ops:
  0.6 1.1 %pack.1 = (bf16[128,512]{1,0:T(8,128)(2,1)S(1)}, bf16[128,512]{1,0:T(8,128)(2,1)S(1)}, bf16[128,512]{1,0:T(8,128)(2,1)S(1)}, bf16[400,512]{1,0:T(8,128)(2,1)S(1)}) custom-call(s32[3,128]{1,0:T(4,128)} %bitcast.14, bf16[3,128,512]{2,1,0:T(8,128)(2,1)} %tokens.1, bf16[1,4,512]{2,1,0:T(4,128)(2,1)} %extra.1), custom_call_target="tpu_custom_call" | custom-call | tf_op jit(solution)/shard_map/pack/pallas_call | solution.py:531
  1.7 3.7 %collective-permute-start = (bf16[128,512]{1,0:T(8,128)(2,1)S(1)}, bf16[128,512]{1,0:T(8,128)(2,1)S(1)}, u32[]{:S(2)}, u32[]{:S(2)}) collective-permute-start(bf16[128,512]{1,0:T(8,128)(2,1)S(1)} %get-tuple-element.29), channel_id=1, source_target_pairs={{0,4},{2,6},{4,0},{6,2},{8,12},{10,14},{12,8},{14,10},{16,20},{18,... | collective-permute-start | bytes 393224 | tf_op jit(solution)/shard_map/ppermute | solution.py:33
  5.4 0.3 collective-permute-start.1
  5.7 0.6 %collective-permute-start.2 = (bf16[128,512]{1,0:T(8,128)(2,1)S(1)}, bf16[128,512]{1,0:T(8,128)(2,1)S(1)}, u32[]{:S(2)}, u32[]{:S(2)}) collective-permute-start(bf16[128,512]{1,0:T(8,128)(2,1)S(1)} %get-tuple-element.31), channel_id=1, source_target_pairs={{0,6},{2,4},{4,2},{6,0},{8,14},{10,12},{12,10},{14,8},{16,22},{18,... | collective-permute-start | bytes 393224 | tf_op jit(solution)/shard_map/ppermute | solution.py:33
  6.3 4.9 %all-gather = bf16[800,512]{1,0:T(8,128)(2,1)S(1)} all-gather(bf16[400,512]{1,0:T(8,128)(2,1)S(1)} %get-tuple-element.25), channel_id=2, replica_groups=mesh['clip'=128,'mp'=2] {'mp'}, dimensions={0}, use_global_device_ids=true | all-gather | bytes 1228800 | tf_op jit(solution)/shard_map/all_gather | solution.py:548
  11.2 0.4 collective-permute-start.6
  11.5 2.4 %ready.1 = (bf16[3,1024,512]{2,1,0:T(8,128)(2,1)S(1)}, bf16[144,512]{1,0:T(8,128)(2,1)S(1)}, bf16[144,512]{1,0:T(8,128)(2,1)S(1)}, bf16[4,128,144]{2,1,0:T(8,128...) custom-call(s32[3,128]{1,0:T(4,128)} %bitcast.15, s32[128]{0:T(128)} %all_lengths.1, s32[128]{0:T(128)} %all_videos.1, ...), custom_call_target="tpu_custom_call" | custom-call | flops 450000000 | bytes 4000000 | tf_op jit(solution)/shard_map/ready/pallas_call | solution.py:416
  14.0 0.0 collective-permute-done
  14.0 0.0 collective-permute-done.1
  14.0 0.0 collective-permute-done.2
  14.1 2.4 %all-gather.1 = bf16[768,512]{1,0:T(8,128)(2,1)S(1)} all-gather(bf16[384,512]{1,0:T(8,128)(2,1)S(1)} %pad_maximum_fusion), channel_id=3, replica_groups=mesh['clip'=128,'mp'=2] {'mp'}, dimensions={0}, use_global_device_ids=true | all-gather | bytes 1179648 | tf_op jit(solution)/shard_map/all_gather | solution.py:554
  16.4 0.0 copy-start.2
  16.4 2.9 %attend.1 = (bf16[128,512]{1,0:T(8,128)(2,1)S(1)}, bf16[128,512]{1,0:T(8,128)(2,1)S(1)}, bf16[768,512]{1,0:T(8,128)(2,1)S(1)}, bf16[768,512]{1,0:T(8,128)(2,1)S(1)}, bf16[4,144,768]{2,1,0:T(8,128)(2,1)S(1)}) custom-call(s32[1,8]{1,0:T(1,128)S(1)} %get-tuple-element.27.facts, f32[1,1024]{1,0:T(1,128)S(1)} %get-tuple-element.28.gain, ...), custom_call_target="tpu_custom_call" | custom-call | flops 1800000000 | bytes 6000000 | tf_op jit(solution)/shard_map/attend/pallas_call | solution.py:448
  19.3 0.0 copy-start
  19.3 0.0 copy-start.1
  19.4 0.0 copy-start.3
  19.4 0.0 copy-start.4
  19.4 1.5 %collective-permute-start.3 = (bf16[128,512]{1,0:T(8,128)(2,1)S(1)}, bf16[128,512]{1,0:T(8,128)(2,1)S(1)}, u32[]{:S(2)}, u32[]{:S(2)}) collective-permute-start(bf16[128,512]{1,0:T(8,128)(2,1)S(1)} %get-tuple-element.40), channel_id=1, source_target_pairs={{0,4},{2,6},{4,0},{6,2},{8,12},{10,14},{12,8},{14,10},{16,20},{18,... | collective-permute-start | bytes 393224 | tf_op jit(solution)/shard_map/ppermute | solution.py:33
  20.9 2.0 %rest.1 = (bf16[128,512]{1,0:T(8,128)(2,1)S(1)}, bf16[144,512]{1,0:T(8,128)(2,1)S(1)}) custom-call(bf16[768,512]{1,0:T(8,128)(2,1)S(1)} %get-tuple-element.36.query, bf16[768,512]{1,0:T(8,128)(2,1)S(1)} %get-tuple-element.37.keys, bf16[4,144,768]{2,1,0:T(8,128)(2,1)S(1)} %get-tuple-element.38.values, s32[1,8]{1,0:T(1,128)S(1)} %get-tuple-element.27.facts), custom_call_target="tpu_custom_call" | custom-call | flops 700000000 | bytes 3000000 | tf_op jit(solution)/shard_map/rest/pallas_call | solution.py:474
  22.9 1.2 %collective-permute-start.4 = (bf16[128,512]{1,0:T(8,128)(2,1)S(1)}, bf16[128,512]{1,0:T(8,128)(2,1)S(1)}, u32[]{:S(2)}, u32[]{:S(2)}) collective-permute-start(bf16[128,512]{1,0:T(8,128)(2,1)S(1)} %get-tuple-element.43), channel_id=1, source_target_pairs={{0,2},{2,0},{4,6},{6,4},{8,10},{10,8},{12,14},{14,12},{16,18},{18,... | collective-permute-start | bytes 393224 | tf_op jit(solution)/shard_map/ppermute | solution.py:33
  24.1 1.5 %collective-permute-start.5 = (bf16[128,512]{1,0:T(8,128)(2,1)S(1)}, bf16[128,512]{1,0:T(8,128)(2,1)S(1)}, u32[]{:S(2)}, u32[]{:S(2)}) collective-permute-start(bf16[128,512]{1,0:T(8,128)(2,1)S(1)} %get-tuple-element.44), channel_id=1, source_target_pairs={{0,6},{2,4},{4,2},{6,0},{8,14},{10,12},{12,10},{14,8},{16,22},{18,... | collective-permute-start | bytes 393224 | tf_op jit(solution)/shard_map/ppermute | solution.py:33
  25.6 0.2 collective-permute-done.3
  25.9 2.7 %all-gather.2 = bf16[288,512]{1,0:T(8,128)(2,1)S(1)} all-gather(bf16[144,512]{1,0:T(8,128)(2,1)S(1)} %get-tuple-element.41), channel_id=4, replica_groups=mesh['clip'=128,'mp'=2] {'mp'}, dimensions={0}, use_global_device_ids=true | all-gather | bytes 442368 | tf_op jit(solution)/shard_map/all_gather | solution.py:562
  28.5 0.0 collective-permute-done.4
  28.5 0.6 %collective-permute-done.5 = bf16[128,512]{1,0:T(8,128)(2,1)S(1)} collective-permute-done((bf16[128,512]{1,0:T(8,128)(2,1)S(1)}, bf16[128,512]{1,0:T(8,128)(2,1)S(1)}, u32[]{:S(2)}, u32[]{:S(2)}) %collective-permute-start.5) | collective-permute-done | bytes 131104 | tf_op jit(solution)/shard_map/ppermute | solution.py:33
  29.2 4.1 %all-gather.3 = bf16[768,512]{1,0:T(8,128)(2,1)S(1)} all-gather(bf16[384,512]{1,0:T(8,128)(2,1)S(1)} %pad_maximum_fusion.1), channel_id=5, replica_groups=mesh['clip'=128,'mp'=2] {'mp'}, dimensions={0}, use_global_device_ids=true | all-gather | bytes 1179648 | tf_op jit(solution)/shard_map/all_gather | solution.py:563
  33.3 0.0 collective-permute-done.6.w_out_other
  33.3 0.0 copy-done.2
  33.3 0.0 copy-done
  33.3 0.0 copy-done.1
  33.3 0.0 copy-done.3
  33.3 0.0 copy-done.4
  33.3 5.9 %feed.1 = (f32[400,512]{1,0:T(8,128)S(1)}, bf16[400,512]{1,0:T(8,128)(2,1)S(1)}) custom-call(s32[3,128]{1,0:T(4,128)S(1)} %bitcast.16, bf16[2,400,512]{2,1,0:T(8,128)(2,1)S(1)} %bitcast.9, bf16[2,144,512]{2,1,0:T(8,128)(2,1)S(1)} %bitcast.13, bf16[2,384,512]{2,1,0:T(8,128)(2,1)S(1)} %bitcast.12, bf16[512,1024]{1,0:T(8,128)(2,1)S(1)} %copy-done.3, ...), custom_call_target="tpu_custom_call" | custom-call | flops 4100000000 | bytes 14000000 | tf_op jit(solution)/shard_map/feed/pallas_call | solution.py:494
  39.2 2.4 %all-gather.4 = bf16[800,512]{1,0:T(8,128)(2,1)S(1)} all-gather(bf16[400,512]{1,0:T(8,128)(2,1)S(1)} %get-tuple-element.47), channel_id=6, replica_groups=mesh['clip'=128,'mp'=2] {'mp'}, dimensions={0}, use_global_device_ids=true | all-gather | bytes 1228800 | tf_op jit(solution)/shard_map/all_gather | solution.py:568
  41.6 0.9 %finish.1 = (bf16[3,128,512]{2,1,0:T(8,128)(2,1)}, bf16[1,4,512]{2,1,0:T(4,128)(2,1)}) custom-call(f32[400,512]{1,0:T(8,128)S(1)} %get-tuple-element.46.base, bf16[2,400,512]{2,1,0:T(8,128)(2,1)S(1)} %bitcast.10), custom_call_target="tpu_custom_call" | custom-call | tf_op jit(solution)/shard_map/finish/pallas_call | solution.py:570
  (2 shorter events, 0.1 us)
Async XLA Ops:
  1.7 12.3 %collective-permute-start = (bf16[128,512]{1,0:T(8,128)(2,1)S(1)}, bf16[128,512]{1,0:T(8,128)(2,1)S(1)}, u32[]{:S(2)}, u32[]{:S(2)}) collective-permute-start(bf16[128,512]{1,0:T(8,128)(2,1)S(1)} %get-tuple-element.29), channel_id=1, source_target_pairs={{0,4},{2,6},{4,0},{6,2},{8,12},{10,14},{12,8},{14,10},{16,20},{18,... | collective-permute-start | bytes 393224 | tf_op jit(solution)/shard_map/ppermute | solution.py:33
  5.4 8.6 %collective-permute-start.1 = (bf16[128,512]{1,0:T(8,128)(2,1)S(1)}, bf16[128,512]{1,0:T(8,128)(2,1)S(1)}, u32[]{:S(2)}, u32[]{:S(2)}) collective-permute-start(bf16[128,512]{1,0:T(8,128)(2,1)S(1)} %get-tuple-element.30), channel_id=1, source_target_pairs={{0,2},{2,0},{4,6},{6,4},{8,10},{10,8},{12,14},{14,12},{16,18},{18,... | collective-permute-start | bytes 393224 | tf_op jit(solution)/shard_map/ppermute | solution.py:33
  5.7 8.3 %collective-permute-start.2 = (bf16[128,512]{1,0:T(8,128)(2,1)S(1)}, bf16[128,512]{1,0:T(8,128)(2,1)S(1)}, u32[]{:S(2)}, u32[]{:S(2)}) collective-permute-start(bf16[128,512]{1,0:T(8,128)(2,1)S(1)} %get-tuple-element.31), channel_id=1, source_target_pairs={{0,6},{2,4},{4,2},{6,0},{8,14},{10,12},{12,10},{14,8},{16,22},{18,... | collective-permute-start | bytes 393224 | tf_op jit(solution)/shard_map/ppermute | solution.py:33
  11.2 22.1 %collective-permute-start.6 = (bf16[512,1024]{1,0:T(8,128)(2,1)}, bf16[512,1024]{1,0:T(8,128)(2,1)S(1)}, u32[]{:S(2)}, u32[]{:S(2)}) collective-permute-start(bf16[512,1024]{1,0:T(8,128)(2,1)} %w_out.1), channel_id=1, source_target_pairs={{0,1},{1,0},{2,3},{3,2},{4,5},{5,4},{6,7},{7,6},{8,9},{9,8},{10,11... | collective-permute-start | bytes 3145736 | tf_op jit(solution)/shard_map/ppermute | solution.py:550
  16.4 16.8 %copy-start.2 = (bf16[2048,1024]{1,0:T(8,128)(2,1)S(1)}, bf16[2048,1024]{1,0:T(8,128)(2,1)}, u32[]{:S(2)}) copy-start(bf16[2048,1024]{1,0:T(8,128)(2,1)} %w_down.1) | copy-start | bytes 12582916
  19.3 13.9 %copy-start = (s32[128,3]{0,1:T(4,128)S(1)}, s32[128,3]{0,1:T(4,128)}, u32[]{:S(2)}) copy-start(s32[128,3]{0,1:T(4,128)} %param.15) | copy-start | bytes 4612
  19.3 13.9 %copy-start.1 = (bf16[1024,2048]{1,0:T(8,128)(2,1)S(1)}, bf16[1024,2048]{1,0:T(8,128)(2,1)}, u32[]{:S(2)}) copy-start(bf16[1024,2048]{1,0:T(8,128)(2,1)} %w_up.1) | copy-start | bytes 12582916
  19.4 13.9 %copy-start.3 = (bf16[512,1024]{1,0:T(8,128)(2,1)S(1)}, bf16[512,1024]{1,0:T(8,128)(2,1)}, u32[]{:S(2)}) copy-start(bf16[512,1024]{1,0:T(8,128)(2,1)} %w_out.1) | copy-start | bytes 3145732
  19.4 13.9 %copy-start.4 = (f32[1024]{0:T(1024)S(1)}, f32[1024]{0:T(1024)}, u32[]{:S(2)}) copy-start(f32[1024]{0:T(1024)} %param.19) | copy-start | bytes 12292
  19.4 6.5 %collective-permute-start.3 = (bf16[128,512]{1,0:T(8,128)(2,1)S(1)}, bf16[128,512]{1,0:T(8,128)(2,1)S(1)}, u32[]{:S(2)}, u32[]{:S(2)}) collective-permute-start(bf16[128,512]{1,0:T(8,128)(2,1)S(1)} %get-tuple-element.40), channel_id=1, source_target_pairs={{0,4},{2,6},{4,0},{6,2},{8,12},{10,14},{12,8},{14,10},{16,20},{18,... | collective-permute-start | bytes 393224 | tf_op jit(solution)/shard_map/ppermute | solution.py:33
  22.9 5.6 %collective-permute-start.4 = (bf16[128,512]{1,0:T(8,128)(2,1)S(1)}, bf16[128,512]{1,0:T(8,128)(2,1)S(1)}, u32[]{:S(2)}, u32[]{:S(2)}) collective-permute-start(bf16[128,512]{1,0:T(8,128)(2,1)S(1)} %get-tuple-element.43), channel_id=1, source_target_pairs={{0,2},{2,0},{4,6},{6,4},{8,10},{10,8},{12,14},{14,12},{16,18},{18,... | collective-permute-start | bytes 393224 | tf_op jit(solution)/shard_map/ppermute | solution.py:33
  24.1 5.0 %collective-permute-start.5 = (bf16[128,512]{1,0:T(8,128)(2,1)S(1)}, bf16[128,512]{1,0:T(8,128)(2,1)S(1)}, u32[]{:S(2)}, u32[]{:S(2)}) collective-permute-start(bf16[128,512]{1,0:T(8,128)(2,1)S(1)} %get-tuple-element.44), channel_id=1, source_target_pairs={{0,6},{2,4},{4,2},{6,0},{8,14},{10,12},{12,10},{14,8},{16,22},{18,... | collective-permute-start | bytes 393224 | tf_op jit(solution)/shard_map/ppermute | solution.py:33
where the time goes:
time: 43.2 us; the launch traced here: 42.5 us
  blocking collectives  16.4 us (38%)
  Pallas kernels  15.2 us (35%)
  starting transfers between devices  9.1 us (21%)
  waiting for transfers between devices  0.85 us (2%)
  between operations  0.77 us (2%)
    ppermute x6, starting transfers between devices, partner(): lax.ppermute(x, 'clip', [(i, i ^ step) for i in range(lax.axis_size('clip...  8.73 us
    all_gather x2, blocking collectives, body(): lax.all_gather(jnp.concatenate([far, near, across], axis=0), 'mp', axis=0)  6.46 us
    pallas_call x1, Pallas kernels, feed(): pl.pallas_call(feed_kernel, name='feed', out_shape=(spec((ROWS, width), F...  5.92 us
    all_gather x1, blocking collectives, body(): stored_all = lax.all_gather(stored, 'mp', axis=0)  4.9 us
    pallas_call x1, Pallas kernels, attend(): pl.pallas_call(attend_kernel, name='attend', out_shape=(block, block, spe...  2.9 us
    all_gather x1, blocking collectives, body(): own_all = lax.all_gather(own, 'mp', axis=0)  2.66 us
    pallas_call x1, Pallas kernels, ready(): pl.pallas_call(ready_kernel, name='ready', out_shape=(spec(w_qkv.shape),...  2.45 us
    all_gather x1, blocking collectives, body(): sums = lax.all_gather(send, 'mp', axis=0)  2.39 us
  transfers between devices with their start and end apart: 7, of which 2 were waited for; matrix products, arithmetic and copies ran while one was open for 0% of the time, Pallas kernels for 17%

commit v1 on v0

--- a/solution.py
+++ b/solution.py
@@ -191,7 +191,7 @@
 
 def visit_blocks(info, places, query, keys, values, context):
     def visit(i, carry):
-        place = places[0] + i * (places[1] - places[0])
+        place = places[0] + i * (places[-1] - places[0])
         block = info[0, place]
         length = info[0, GROUP]
         video = info[0, GROUP + 1]
@@ -206,7 +206,7 @@
 
         return carry
 
-    lax.fori_loop(0, 2, visit, 0)
+    lax.fori_loop(0, len(places), visit, 0)
 
 
 def attend_kernel(
@@ -279,7 +279,16 @@
     across[...] = context[1]
 
 
-def rest_kernel(query, keys, values, facts, near, own, context, info, sems):
+def near_kernel(query, keys, values, facts, near, context, info, sems):
+    load = pltpu.make_async_copy(facts, info, sems.at[0])
+    load.start()
+    context[...] = jnp.zeros_like(context)
+    load.wait()
+    visit_blocks(info, (1,), query, keys, values, context)
+    near[...] = context[0]
+
+
+def own_kernel(query, keys, values, facts, own, context, info, sems):
     load = pltpu.make_async_copy(facts, info, sems.at[0])
     load.start()
     width = query.shape[1]
@@ -288,9 +297,8 @@
     load.wait()
     length = info[0, GROUP]
     video = info[0, GROUP + 1]
-    visit_blocks(info, (1, 3), query, keys, values, context)
-    near[...] = context[0]
-    own[:BLK, :] = context[1]
+    visit_blocks(info, (GROUP - 1,), query, keys, values, context)
+    own[:BLK, :] = context[0]
 
     heads = width // HEAD_DIM
     sub = 8
@@ -468,22 +476,21 @@
     )(facts, gain, arrived, weights, *own_qkv)
 
 
-def rest(query, keys, values, facts):
+def part(kernel, name, rows, query, keys, values, facts):
     width = query.shape[1]
-    info = (1, 2 * GROUP)
     return pl.pallas_call(
-        rest_kernel,
-        name="rest",
-        out_shape=(spec((BLK, width)), spec((BLK + PAD, width))),
+        kernel,
+        name=name,
+        out_shape=spec((rows, width)),
         in_specs=[VMEM] * 4,
-        out_specs=(VMEM,) * 2,
+        out_specs=VMEM,
         scratch_shapes=[
-            pltpu.VMEM((2, BLK, width), BF16),
-            pltpu.SMEM(info, jnp.int32),
+            pltpu.VMEM((1, BLK, width), BF16),
+            pltpu.SMEM(facts.shape, jnp.int32),
             DMA((1,)),
         ],
         compiler_params=pltpu.CompilerParams(vmem_limit_bytes=16 << 20),
-        cost_estimate=pl.CostEstimate(flops=700000000, bytes_accessed=3000000, transcendentals=1500000),
+        cost_estimate=pl.CostEstimate(flops=400000000, bytes_accessed=3000000, transcendentals=700000),
     )(query, keys, values, facts)
 
 
@@ -556,9 +563,10 @@
     far, across, query, keys, values = attend(facts, gain, arrived, weights, own_qkv)
     far = partner(far, 2)
     across = partner(across, 3)
-    near, own = rest(query, keys, values, facts)
+    near = part(near_kernel, "near", BLK, query, keys, values, facts)
     near = partner(near, 1)
-    own, far = lax.optimization_barrier((own, far))
+    facts, far = lax.optimization_barrier((facts, far))
+    own = part(own_kernel, "own", BLK + PAD, query, keys, values, facts)
     own_all = lax.all_gather(own, "mp", axis=0)
     arrived = lax.all_gather(jnp.concatenate([far, near, across], axis=0), "mp", axis=0)
 

time: 43.2 us -> 43.7 us (1.012)
  Pallas kernels: 15.2 us -> 16.8 us
  blocking collectives: 16.4 us -> 15.3 us
  waiting for transfers between devices: 0.85 us -> 1.7 us
  starting transfers between devices: 9.1 us -> 8.52 us
    all_gather x2, blocking collectives: 6.46 us -> 4.74 us  [body(): lax.all_gather(jnp.concatenate([far, near, across], axis=0), 'mp', axis=0)]
    pallas_call x1 -> x2, Pallas kernels: 2.04 us -> 3.53 us  [part(): pl.pallas_call(kernel, name=name, out_shape=spec((rows, width)), in_specs...]
    ppermute x6, waiting for transfers between devices: 0.85 us -> 1.7 us  [partner(): lax.ppermute(x, 'clip', [(i, i ^ step) for i in range(lax.axis_size('clip...]
    all_gather x1, blocking collectives: 2.66 us -> 3.28 us  [body(): own_all = lax.all_gather(own, 'mp', axis=0)]
    ppermute x6, starting transfers between devices: 8.73 us -> 8.15 us  [partner(): lax.ppermute(x, 'clip', [(i, i ^ step) for i in range(lax.axis_size('clip...]
  transfers between devices with their start and end apart: 7 -> 7, of which waited for: 2 -> 1; matrix products, arithmetic and copies ran while one was open for 0% -> 0% of each run, Pallas kernels for 17% -> 21%
where the time goes in v1:
time: 43.7 us; the launch traced here: 43.2 us
  Pallas kernels  16.8 us (38%)
  blocking collectives  15.3 us (35%)
  starting transfers between devices  8.52 us (19%)
  waiting for transfers between devices  1.7 us (4%)
  between operations  0.79 us (2%)
    ppermute x6, starting transfers between devices, partner(): lax.ppermute(x, 'clip', [(i, i ^ step) for i in range(lax.axis_size('clip...  8.15 us
    pallas_call x1, Pallas kernels, feed(): pl.pallas_call(feed_kernel, name='feed', out_shape=(spec((ROWS, width), F...  5.74 us
    all_gather x1, blocking collectives, body(): stored_all = lax.all_gather(stored, 'mp', axis=0)  4.9 us
    all_gather x2, blocking collectives, body(): lax.all_gather(jnp.concatenate([far, near, across], axis=0), 'mp', axis=0)  4.74 us
    pallas_call x2, Pallas kernels, part(): pl.pallas_call(kernel, name=name, out_shape=spec((rows, width)), in_specs...  3.53 us
    all_gather x1, blocking collectives, body(): own_all = lax.all_gather(own, 'mp', axis=0)  3.28 us
    pallas_call x1, Pallas kernels, attend(): pl.pallas_call(attend_kernel, name='attend', out_shape=(block, block, spe...  3.09 us
    pallas_call x1, Pallas kernels, ready(): pl.pallas_call(ready_kernel, name='ready', out_shape=(spec(w_qkv.shape),...  2.45 us
  transfers between devices with their start and end apart: 7, of which 1 were waited for; matrix products, arithmetic and copies ran while one was open for 0% of the time, Pallas kernels for 21%

profile of v1, /device:TPU:1, one launch (start us, length us, event | category | flops | bytes accessed | tf_op | source)
XLA Modules:
  0.0 43.2 jit_solution(13518049628318993469)
XLA Ops:
  0.6 1.1 %pack.1 = (bf16[128,512]{1,0:T(8,128)(2,1)S(1)}, bf16[128,512]{1,0:T(8,128)(2,1)S(1)}, bf16[128,512]{1,0:T(8,128)(2,1)S(1)}, bf16[400,512]{1,0:T(8,128)(2,1)S(1)}) custom-call(s32[3,128]{1,0:T(4,128)} %bitcast.14, bf16[3,128,512]{2,1,0:T(8,128)(2,1)} %tokens.1, bf16[1,4,512]{2,1,0:T(4,128)(2,1)} %extra.1), custom_call_target="tpu_custom_call" | custom-call | tf_op jit(solution)/shard_map/pack/pallas_call | solution.py:538
  1.7 3.7 %collective-permute-start = (bf16[128,512]{1,0:T(8,128)(2,1)S(1)}, bf16[128,512]{1,0:T(8,128)(2,1)S(1)}, u32[]{:S(2)}, u32[]{:S(2)}) collective-permute-start(bf16[128,512]{1,0:T(8,128)(2,1)S(1)} %get-tuple-element.27), channel_id=1, source_target_pairs={{0,4},{2,6},{4,0},{6,2},{8,12},{10,14},{12,8},{14,10},{16,20},{18,... | collective-permute-start | bytes 393224 | tf_op jit(solution)/shard_map/ppermute | solution.py:33
  5.4 0.3 collective-permute-start.1
  5.7 0.6 %collective-permute-start.2 = (bf16[128,512]{1,0:T(8,128)(2,1)S(1)}, bf16[128,512]{1,0:T(8,128)(2,1)S(1)}, u32[]{:S(2)}, u32[]{:S(2)}) collective-permute-start(bf16[128,512]{1,0:T(8,128)(2,1)S(1)} %get-tuple-element.29), channel_id=1, source_target_pairs={{0,6},{2,4},{4,2},{6,0},{8,14},{10,12},{12,10},{14,8},{16,22},{18,... | collective-permute-start | bytes 393224 | tf_op jit(solution)/shard_map/ppermute | solution.py:33
  6.3 4.9 %all-gather = bf16[800,512]{1,0:T(8,128)(2,1)S(1)} all-gather(bf16[400,512]{1,0:T(8,128)(2,1)S(1)} %get-tuple-element.23), channel_id=2, replica_groups=mesh['clip'=128,'mp'=2] {'mp'}, dimensions={0}, use_global_device_ids=true | all-gather | bytes 1228800 | tf_op jit(solution)/shard_map/all_gather | solution.py:555
  11.2 0.4 collective-permute-start.6
  11.5 2.4 %ready.1 = (bf16[3,1024,512]{2,1,0:T(8,128)(2,1)S(1)}, bf16[144,512]{1,0:T(8,128)(2,1)S(1)}, bf16[144,512]{1,0:T(8,128)(2,1)S(1)}, bf16[4,128,144]{2,1,0:T(8,128...) custom-call(s32[3,128]{1,0:T(4,128)} %bitcast.15, s32[128]{0:T(128)} %all_lengths.1, s32[128]{0:T(128)} %all_videos.1, ...), custom_call_target="tpu_custom_call" | custom-call | flops 450000000 | bytes 4000000 | tf_op jit(solution)/shard_map/ready/pallas_call | solution.py:424
  14.0 0.0 collective-permute-done
  14.0 0.0 collective-permute-done.1
  14.0 0.0 collective-permute-done.2
  14.1 2.4 %all-gather.1 = bf16[768,512]{1,0:T(8,128)(2,1)S(1)} all-gather(bf16[384,512]{1,0:T(8,128)(2,1)S(1)} %pad_maximum_fusion), channel_id=3, replica_groups=mesh['clip'=128,'mp'=2] {'mp'}, dimensions={0}, use_global_device_ids=true | all-gather | bytes 1179648 | tf_op jit(solution)/shard_map/all_gather | solution.py:561
  16.4 0.0 copy-start.2
  16.4 3.1 %attend.1 = (bf16[128,512]{1,0:T(8,128)(2,1)S(1)}, bf16[128,512]{1,0:T(8,128)(2,1)S(1)}, bf16[768,512]{1,0:T(8,128)(2,1)S(1)}, bf16[768,512]{1,0:T(8,128)(2,1)S(1)}, bf16[4,144,768]{2,1,0:T(8,128)(2,1)S(1)}) custom-call(s32[1,8]{1,0:T(1,128)S(1)} %get-tuple-element.38.facts, f32[1,1024]{1,0:T(1,128)S(1)} %get-tuple-element.26.gain, ...), custom_call_target="tpu_custom_call" | custom-call | flops 1800000000 | bytes 6000000 | tf_op jit(solution)/shard_map/attend/pallas_call | solution.py:456
  19.5 0.0 copy-start
  19.5 0.0 copy-start.1
  19.5 0.0 copy-start.3
  19.6 0.0 copy-start.4
  19.6 2.1 %collective-permute-start.3 = (bf16[128,512]{1,0:T(8,128)(2,1)S(1)}, bf16[128,512]{1,0:T(8,128)(2,1)S(1)}, u32[]{:S(2)}, u32[]{:S(2)}) collective-permute-start(bf16[128,512]{1,0:T(8,128)(2,1)S(1)} %get-tuple-element.37), channel_id=1, source_target_pairs={{0,4},{2,6},{4,0},{6,2},{8,12},{10,14},{12,8},{14,10},{16,20},{18,... | collective-permute-start | bytes 393224 | tf_op jit(solution)/shard_map/ppermute | solution.py:33
  21.6 1.2 %near.1 = bf16[128,512]{1,0:T(8,128)(2,1)S(1)} custom-call(bf16[768,512]{1,0:T(8,128)(2,1)S(1)} %get-tuple-element.34.query, bf16[768,512]{1,0:T(8,128)(2,1)S(1)} %get-tuple-element.35.keys, bf16[4,144,768]{2,1,0:T(8,128)(2,1)S(1)} %get-tuple-element.36.values, s32[1,8]{1,0:T(1,128)S(1)} %get-tuple-element.38.facts), custom_call_target="tpu_custom_call" | custom-call | flops 400000000 | bytes 3000000 | tf_op jit(solution)/shard_map/near/pallas_call | solution.py:481
  22.8 0.1 collective-permute-start.4
  22.9 1.5 %collective-permute-start.5 = (bf16[128,512]{1,0:T(8,128)(2,1)S(1)}, bf16[128,512]{1,0:T(8,128)(2,1)S(1)}, u32[]{:S(2)}, u32[]{:S(2)}) collective-permute-start(bf16[128,512]{1,0:T(8,128)(2,1)S(1)} %get-tuple-element.40), channel_id=1, source_target_pairs={{0,6},{2,4},{4,2},{6,0},{8,14},{10,12},{12,10},{14,8},{16,22},{18,... | collective-permute-start | bytes 393224 | tf_op jit(solution)/shard_map/ppermute | solution.py:33
  24.4 1.7 %collective-permute-done.3 = bf16[128,512]{1,0:T(8,128)(2,1)S(1)} collective-permute-done((bf16[128,512]{1,0:T(8,128)(2,1)S(1)}, bf16[128,512]{1,0:T(8,128)(2,1)S(1)}, u32[]{:S(2)}, u32[]{:S(2)}) %collective-permute-start.3) | collective-permute-done | bytes 131104 | tf_op jit(solution)/shard_map/ppermute | solution.py:33
  26.1 2.4 %own.1 = bf16[144,512]{1,0:T(8,128)(2,1)S(1)} custom-call(bf16[768,512]{1,0:T(8,128)(2,1)S(1)} %get-tuple-element.34.query, bf16[768,512]{1,0:T(8,128)(2,1)S(1)} %get-tuple-element.35.keys, bf16[4,144,768]{2,1,0:T(8,128)(2,1)S(1)} %get-tuple-element.36.values, s32[1,8]{1,0:T(1,128)S(1)} %get-tuple-element.38.facts), custom_call_target="tpu_custom_call" | custom-call | flops 400000000 | bytes 3000000 | tf_op jit(solution)/shard_map/own/pallas_call | solution.py:481
  28.4 3.3 %all-gather.2 = bf16[288,512]{1,0:T(8,128)(2,1)S(1)} all-gather(bf16[144,512]{1,0:T(8,128)(2,1)S(1)} %own.1), channel_id=4, replica_groups=mesh['clip'=128,'mp'=2] {'mp'}, dimensions={0}, use_global_device_ids=true | all-gather | bytes 442368 | tf_op jit(solution)/shard_map/all_gather | solution.py:570
  31.7 0.0 collective-permute-done.4
  31.7 0.0 collective-permute-done.5
  31.8 2.4 %all-gather.3 = bf16[768,512]{1,0:T(8,128)(2,1)S(1)} all-gather(bf16[384,512]{1,0:T(8,128)(2,1)S(1)} %pad_maximum_fusion.1), channel_id=5, replica_groups=mesh['clip'=128,'mp'=2] {'mp'}, dimensions={0}, use_global_device_ids=true | all-gather | bytes 1179648 | tf_op jit(solution)/shard_map/all_gather | solution.py:571
  34.1 0.0 collective-permute-done.6.w_out_other
  34.1 0.0 copy-done.2
  34.1 0.0 copy-done
  34.1 0.0 copy-done.1
  34.1 0.0 copy-done.3
  34.2 0.0 copy-done.4
  34.2 5.7 %feed.1 = (f32[400,512]{1,0:T(8,128)S(1)}, bf16[400,512]{1,0:T(8,128)(2,1)S(1)}) custom-call(s32[3,128]{1,0:T(4,128)S(1)} %bitcast.16, bf16[2,400,512]{2,1,0:T(8,128)(2,1)S(1)} %bitcast.9, bf16[2,144,512]{2,1,0:T(8,128)(2,1)S(1)} %bitcast.13, bf16[2,384,512]{2,1,0:T(8,128)(2,1)S(1)} %bitcast.12, bf16[512,1024]{1,0:T(8,128)(2,1)S(1)} %copy-done.3, ...), custom_call_target="tpu_custom_call" | custom-call | flops 4100000000 | bytes 14000000 | tf_op jit(solution)/shard_map/feed/pallas_call | solution.py:501
  39.9 2.4 %all-gather.4 = bf16[800,512]{1,0:T(8,128)(2,1)S(1)} all-gather(bf16[400,512]{1,0:T(8,128)(2,1)S(1)} %get-tuple-element.43), channel_id=6, replica_groups=mesh['clip'=128,'mp'=2] {'mp'}, dimensions={0}, use_global_device_ids=true | all-gather | bytes 1228800 | tf_op jit(solution)/shard_map/all_gather | solution.py:576
  42.3 0.9 %finish.1 = (bf16[3,128,512]{2,1,0:T(8,128)(2,1)}, bf16[1,4,512]{2,1,0:T(4,128)(2,1)}) custom-call(f32[400,512]{1,0:T(8,128)S(1)} %get-tuple-element.42.base, bf16[2,400,512]{2,1,0:T(8,128)(2,1)S(1)} %bitcast.10), custom_call_target="tpu_custom_call" | custom-call | tf_op jit(solution)/shard_map/finish/pallas_call | solution.py:578
  (2 shorter events, 0.1 us)
Async XLA Ops:
  1.7 12.3 %collective-permute-start = (bf16[128,512]{1,0:T(8,128)(2,1)S(1)}, bf16[128,512]{1,0:T(8,128)(2,1)S(1)}, u32[]{:S(2)}, u32[]{:S(2)}) collective-permute-start(bf16[128,512]{1,0:T(8,128)(2,1)S(1)} %get-tuple-element.27), channel_id=1, source_target_pairs={{0,4},{2,6},{4,0},{6,2},{8,12},{10,14},{12,8},{14,10},{16,20},{18,... | collective-permute-start | bytes 393224 | tf_op jit(solution)/shard_map/ppermute | solution.py:33
  5.4 8.6 %collective-permute-start.1 = (bf16[128,512]{1,0:T(8,128)(2,1)S(1)}, bf16[128,512]{1,0:T(8,128)(2,1)S(1)}, u32[]{:S(2)}, u32[]{:S(2)}) collective-permute-start(bf16[128,512]{1,0:T(8,128)(2,1)S(1)} %get-tuple-element.28), channel_id=1, source_target_pairs={{0,2},{2,0},{4,6},{6,4},{8,10},{10,8},{12,14},{14,12},{16,18},{18,... | collective-permute-start | bytes 393224 | tf_op jit(solution)/shard_map/ppermute | solution.py:33
  5.7 8.3 %collective-permute-start.2 = (bf16[128,512]{1,0:T(8,128)(2,1)S(1)}, bf16[128,512]{1,0:T(8,128)(2,1)S(1)}, u32[]{:S(2)}, u32[]{:S(2)}) collective-permute-start(bf16[128,512]{1,0:T(8,128)(2,1)S(1)} %get-tuple-element.29), channel_id=1, source_target_pairs={{0,6},{2,4},{4,2},{6,0},{8,14},{10,12},{12,10},{14,8},{16,22},{18,... | collective-permute-start | bytes 393224 | tf_op jit(solution)/shard_map/ppermute | solution.py:33
  11.2 23.0 %collective-permute-start.6 = (bf16[512,1024]{1,0:T(8,128)(2,1)}, bf16[512,1024]{1,0:T(8,128)(2,1)S(1)}, u32[]{:S(2)}, u32[]{:S(2)}) collective-permute-start(bf16[512,1024]{1,0:T(8,128)(2,1)} %w_out.1), channel_id=1, source_target_pairs={{0,1},{1,0},{2,3},{3,2},{4,5},{5,4},{6,7},{7,6},{8,9},{9,8},{10,11... | collective-permute-start | bytes 3145736 | tf_op jit(solution)/shard_map/ppermute | solution.py:557
  16.4 17.7 %copy-start.2 = (bf16[2048,1024]{1,0:T(8,128)(2,1)S(1)}, bf16[2048,1024]{1,0:T(8,128)(2,1)}, u32[]{:S(2)}) copy-start(bf16[2048,1024]{1,0:T(8,128)(2,1)} %w_down.1) | copy-start | bytes 12582916
  19.5 14.6 %copy-start = (s32[128,3]{0,1:T(4,128)S(1)}, s32[128,3]{0,1:T(4,128)}, u32[]{:S(2)}) copy-start(s32[128,3]{0,1:T(4,128)} %param.15) | copy-start | bytes 4612
  19.5 14.6 %copy-start.1 = (bf16[1024,2048]{1,0:T(8,128)(2,1)S(1)}, bf16[1024,2048]{1,0:T(8,128)(2,1)}, u32[]{:S(2)}) copy-start(bf16[1024,2048]{1,0:T(8,128)(2,1)} %w_up.1) | copy-start | bytes 12582916
  19.5 14.6 %copy-start.3 = (bf16[512,1024]{1,0:T(8,128)(2,1)S(1)}, bf16[512,1024]{1,0:T(8,128)(2,1)}, u32[]{:S(2)}) copy-start(bf16[512,1024]{1,0:T(8,128)(2,1)} %w_out.1) | copy-start | bytes 3145732
  19.6 14.6 %copy-start.4 = (f32[1024]{0:T(1024)S(1)}, f32[1024]{0:T(1024)}, u32[]{:S(2)}) copy-start(f32[1024]{0:T(1024)} %param.19) | copy-start | bytes 12292
  19.6 6.5 %collective-permute-start.3 = (bf16[128,512]{1,0:T(8,128)(2,1)S(1)}, bf16[128,512]{1,0:T(8,128)(2,1)S(1)}, u32[]{:S(2)}, u32[]{:S(2)}) collective-permute-start(bf16[128,512]{1,0:T(8,128)(2,1)S(1)} %get-tuple-element.37), channel_id=1, source_target_pairs={{0,4},{2,6},{4,0},{6,2},{8,12},{10,14},{12,8},{14,10},{16,20},{18,... | collective-permute-start | bytes 393224 | tf_op jit(solution)/shard_map/ppermute | solution.py:33
  22.8 8.9 %collective-permute-start.4 = (bf16[128,512]{1,0:T(8,128)(2,1)S(1)}, bf16[128,512]{1,0:T(8,128)(2,1)S(1)}, u32[]{:S(2)}, u32[]{:S(2)}) collective-permute-start(bf16[128,512]{1,0:T(8,128)(2,1)S(1)} %near.1), channel_id=1, source_target_pairs={{0,2},{2,0},{4,6},{6,4},{8,10},{10,8},{12,14},{14,12},{16,18},{18,... | collective-permute-start | bytes 393224 | tf_op jit(solution)/shard_map/ppermute | solution.py:33
  22.9 8.8 %collective-permute-start.5 = (bf16[128,512]{1,0:T(8,128)(2,1)S(1)}, bf16[128,512]{1,0:T(8,128)(2,1)S(1)}, u32[]{:S(2)}, u32[]{:S(2)}) collective-permute-start(bf16[128,512]{1,0:T(8,128)(2,1)S(1)} %get-tuple-element.40), channel_id=1, source_target_pairs={{0,6},{2,4},{4,2},{6,0},{8,14},{10,12},{12,10},{14,8},{16,22},{18,... | collective-permute-start | bytes 393224 | tf_op jit(solution)/shard_map/ppermute | solution.py:33

commit v2 on v1

--- a/solution.py
+++ b/solution.py
@@ -565,8 +565,8 @@
     across = partner(across, 3)
     near = part(near_kernel, "near", BLK, query, keys, values, facts)
     near = partner(near, 1)
-    facts, far = lax.optimization_barrier((facts, far))
     own = part(own_kernel, "own", BLK + PAD, query, keys, values, facts)
+    own, far = lax.optimization_barrier((own, far))
     own_all = lax.all_gather(own, "mp", axis=0)
     arrived = lax.all_gather(jnp.concatenate([far, near, across], axis=0), "mp", axis=0)
 

time: 43.7 us -> 41.7 us (0.954)
  waiting for transfers between devices: 1.7 us -> 0.02 us
    ppermute x6, waiting for transfers between devices: 1.7 us -> 0.02 us  [partner(): lax.ppermute(x, 'clip', [(i, i ^ step) for i in range(lax.axis_size('clip...]
    all_gather x1, blocking collectives: 3.28 us -> 2.68 us  [body(): own_all = lax.all_gather(own, 'mp', axis=0)]
    all_gather x2, blocking collectives: 4.74 us -> 5.24 us  [body(): lax.all_gather(jnp.concatenate([far, near, across], axis=0), 'mp', axis=0)]
  transfers between devices with their start and end apart: 7 -> 7, of which waited for: 1 -> 0; matrix products, arithmetic and copies ran while one was open for 0% -> 0% of each run, Pallas kernels for 21% -> 22%
where the time goes in v2:
time: 41.7 us; the launch traced here: 41.3 us
  Pallas kernels  16.8 us (40%)
  blocking collectives  15.2 us (36%)
  starting transfers between devices  8.46 us (20%)
  between operations  0.79 us (2%)
    ppermute x6, starting transfers between devices, partner(): lax.ppermute(x, 'clip', [(i, i ^ step) for i in range(lax.axis_size('clip...  8.08 us
    pallas_call x1, Pallas kernels, feed(): pl.pallas_call(feed_kernel, name='feed', out_shape=(spec((ROWS, width), F...  5.74 us
    all_gather x2, blocking collectives, body(): lax.all_gather(jnp.concatenate([far, near, across], axis=0), 'mp', axis=0)  5.24 us
    all_gather x1, blocking collectives, body(): stored_all = lax.all_gather(stored, 'mp', axis=0)  4.9 us
    pallas_call x2, Pallas kernels, part(): pl.pallas_call(kernel, name=name, out_shape=spec((rows, width)), in_specs...  3.74 us
    pallas_call x1, Pallas kernels, attend(): pl.pallas_call(attend_kernel, name='attend', out_shape=(block, block, spe...  2.89 us
    all_gather x1, blocking collectives, body(): own_all = lax.all_gather(own, 'mp', axis=0)  2.68 us
    pallas_call x1, Pallas kernels, ready(): pl.pallas_call(ready_kernel, name='ready', out_shape=(spec(w_qkv.shape),...  2.45 us
  transfers between devices with their start and end apart: 7, of which 0 were waited for; matrix products, arithmetic and copies ran while one was open for 0% of the time, Pallas kernels for 22%

profile of v2, /device:TPU:1, one launch (start us, length us, event | category | flops | bytes accessed | tf_op | source)
XLA Modules:
  0.0 41.3 jit_solution(10751783375806765982)
XLA Ops:
  0.6 1.1 %pack.1 = (bf16[128,512]{1,0:T(8,128)(2,1)S(1)}, bf16[128,512]{1,0:T(8,128)(2,1)S(1)}, bf16[128,512]{1,0:T(8,128)(2,1)S(1)}, bf16[400,512]{1,0:T(8,128)(2,1)S(1)}) custom-call(s32[3,128]{1,0:T(4,128)} %bitcast.14, bf16[3,128,512]{2,1,0:T(8,128)(2,1)} %tokens.1, bf16[1,4,512]{2,1,0:T(4,128)(2,1)} %extra.1), custom_call_target="tpu_custom_call" | custom-call | tf_op jit(solution)/shard_map/pack/pallas_call | solution.py:538
  1.7 3.7 %collective-permute-start = (bf16[128,512]{1,0:T(8,128)(2,1)S(1)}, bf16[128,512]{1,0:T(8,128)(2,1)S(1)}, u32[]{:S(2)}, u32[]{:S(2)}) collective-permute-start(bf16[128,512]{1,0:T(8,128)(2,1)S(1)} %get-tuple-element.27), channel_id=1, source_target_pairs={{0,4},{2,6},{4,0},{6,2},{8,12},{10,14},{12,8},{14,10},{16,20},{18,... | collective-permute-start | bytes 393224 | tf_op jit(solution)/shard_map/ppermute | solution.py:33
  5.4 0.3 collective-permute-start.1
  5.7 0.6 %collective-permute-start.2 = (bf16[128,512]{1,0:T(8,128)(2,1)S(1)}, bf16[128,512]{1,0:T(8,128)(2,1)S(1)}, u32[]{:S(2)}, u32[]{:S(2)}) collective-permute-start(bf16[128,512]{1,0:T(8,128)(2,1)S(1)} %get-tuple-element.29), channel_id=1, source_target_pairs={{0,6},{2,4},{4,2},{6,0},{8,14},{10,12},{12,10},{14,8},{16,22},{18,... | collective-permute-start | bytes 393224 | tf_op jit(solution)/shard_map/ppermute | solution.py:33
  6.3 4.9 %all-gather = bf16[800,512]{1,0:T(8,128)(2,1)S(1)} all-gather(bf16[400,512]{1,0:T(8,128)(2,1)S(1)} %get-tuple-element.23), channel_id=2, replica_groups=mesh['clip'=128,'mp'=2] {'mp'}, dimensions={0}, use_global_device_ids=true | all-gather | bytes 1228800 | tf_op jit(solution)/shard_map/all_gather | solution.py:555
  11.2 0.4 collective-permute-start.6
  11.5 2.4 %ready.1 = (bf16[3,1024,512]{2,1,0:T(8,128)(2,1)S(1)}, bf16[144,512]{1,0:T(8,128)(2,1)S(1)}, bf16[144,512]{1,0:T(8,128)(2,1)S(1)}, bf16[4,128,144]{2,1,0:T(8,128...) custom-call(s32[3,128]{1,0:T(4,128)} %bitcast.15, s32[128]{0:T(128)} %all_lengths.1, s32[128]{0:T(128)} %all_videos.1, ...), custom_call_target="tpu_custom_call" | custom-call | flops 450000000 | bytes 4000000 | tf_op jit(solution)/shard_map/ready/pallas_call | solution.py:424
  14.0 0.0 collective-permute-done
  14.0 0.0 collective-permute-done.1
  14.0 0.0 collective-permute-done.2
  14.1 2.4 %all-gather.1 = bf16[768,512]{1,0:T(8,128)(2,1)S(1)} all-gather(bf16[384,512]{1,0:T(8,128)(2,1)S(1)} %pad_maximum_fusion), channel_id=3, replica_groups=mesh['clip'=128,'mp'=2] {'mp'}, dimensions={0}, use_global_device_ids=true | all-gather | bytes 1179648 | tf_op jit(solution)/shard_map/all_gather | solution.py:561
  16.4 0.0 copy-start.2
  16.4 2.9 %attend.1 = (bf16[128,512]{1,0:T(8,128)(2,1)S(1)}, bf16[128,512]{1,0:T(8,128)(2,1)S(1)}, bf16[768,512]{1,0:T(8,128)(2,1)S(1)}, bf16[768,512]{1,0:T(8,128)(2,1)S(1)}, bf16[4,144,768]{2,1,0:T(8,128)(2,1)S(1)}) custom-call(s32[1,8]{1,0:T(1,128)S(1)} %get-tuple-element.25.facts, f32[1,1024]{1,0:T(1,128)S(1)} %get-tuple-element.26.gain, ...), custom_call_target="tpu_custom_call" | custom-call | flops 1800000000 | bytes 6000000 | tf_op jit(solution)/shard_map/attend/pallas_call | solution.py:456
  19.3 0.0 copy-start
  19.3 0.0 copy-start.1
  19.3 0.0 copy-start.3
  19.4 0.0 copy-start.4
  19.4 2.2 %collective-permute-start.3 = (bf16[128,512]{1,0:T(8,128)(2,1)S(1)}, bf16[128,512]{1,0:T(8,128)(2,1)S(1)}, u32[]{:S(2)}, u32[]{:S(2)}) collective-permute-start(bf16[128,512]{1,0:T(8,128)(2,1)S(1)} %get-tuple-element.37), channel_id=1, source_target_pairs={{0,4},{2,6},{4,0},{6,2},{8,12},{10,14},{12,8},{14,10},{16,20},{18,... | collective-permute-start | bytes 393224 | tf_op jit(solution)/shard_map/ppermute | solution.py:33
  21.6 1.4 %near.1 = bf16[128,512]{1,0:T(8,128)(2,1)S(1)} custom-call(bf16[768,512]{1,0:T(8,128)(2,1)S(1)} %get-tuple-element.34.query, bf16[768,512]{1,0:T(8,128)(2,1)S(1)} %get-tuple-element.35.keys, bf16[4,144,768]{2,1,0:T(8,128)(2,1)S(1)} %get-tuple-element.36.values, s32[1,8]{1,0:T(1,128)S(1)} %get-tuple-element.25.facts), custom_call_target="tpu_custom_call" | custom-call | flops 400000000 | bytes 3000000 | tf_op jit(solution)/shard_map/near/pallas_call | solution.py:481
  22.9 0.1 collective-permute-start.4
  23.0 1.3 %collective-permute-start.5 = (bf16[128,512]{1,0:T(8,128)(2,1)S(1)}, bf16[128,512]{1,0:T(8,128)(2,1)S(1)}, u32[]{:S(2)}, u32[]{:S(2)}) collective-permute-start(bf16[128,512]{1,0:T(8,128)(2,1)S(1)} %get-tuple-element.40), channel_id=1, source_target_pairs={{0,6},{2,4},{4,2},{6,0},{8,14},{10,12},{12,10},{14,8},{16,22},{18,... | collective-permute-start | bytes 393224 | tf_op jit(solution)/shard_map/ppermute | solution.py:33
  24.3 2.4 %own.1 = bf16[144,512]{1,0:T(8,128)(2,1)S(1)} custom-call(bf16[768,512]{1,0:T(8,128)(2,1)S(1)} %get-tuple-element.34.query, bf16[768,512]{1,0:T(8,128)(2,1)S(1)} %get-tuple-element.35.keys, bf16[4,144,768]{2,1,0:T(8,128)(2,1)S(1)} %get-tuple-element.36.values, s32[1,8]{1,0:T(1,128)S(1)} %get-tuple-element.25.facts), custom_call_target="tpu_custom_call" | custom-call | flops 400000000 | bytes 3000000 | tf_op jit(solution)/shard_map/own/pallas_call | solution.py:481
  26.7 0.0 collective-permute-done.3
  26.7 2.7 %all-gather.2 = bf16[288,512]{1,0:T(8,128)(2,1)S(1)} all-gather(bf16[144,512]{1,0:T(8,128)(2,1)S(1)} %own.1), channel_id=4, replica_groups=mesh['clip'=128,'mp'=2] {'mp'}, dimensions={0}, use_global_device_ids=true | all-gather | bytes 442368 | tf_op jit(solution)/shard_map/all_gather | solution.py:570
  29.4 0.0 collective-permute-done.4
  29.4 0.0 collective-permute-done.5
  29.4 2.9 %all-gather.3 = bf16[768,512]{1,0:T(8,128)(2,1)S(1)} all-gather(bf16[384,512]{1,0:T(8,128)(2,1)S(1)} %pad_maximum_fusion.1), channel_id=5, replica_groups=mesh['clip'=128,'mp'=2] {'mp'}, dimensions={0}, use_global_device_ids=true | all-gather | bytes 1179648 | tf_op jit(solution)/shard_map/all_gather | solution.py:571
  32.3 0.0 collective-permute-done.6.w_out_other
  32.3 0.0 copy-done.2
  32.3 0.0 copy-done
  32.3 0.0 copy-done.1
  32.3 0.0 copy-done.3
  32.3 0.0 copy-done.4
  32.3 5.7 %feed.1 = (f32[400,512]{1,0:T(8,128)S(1)}, bf16[400,512]{1,0:T(8,128)(2,1)S(1)}) custom-call(s32[3,128]{1,0:T(4,128)S(1)} %bitcast.16, bf16[2,400,512]{2,1,0:T(8,128)(2,1)S(1)} %bitcast.9, bf16[2,144,512]{2,1,0:T(8,128)(2,1)S(1)} %bitcast.13, bf16[2,384,512]{2,1,0:T(8,128)(2,1)S(1)} %bitcast.12, bf16[512,1024]{1,0:T(8,128)(2,1)S(1)} %copy-done.3, ...), custom_call_target="tpu_custom_call" | custom-call | flops 4100000000 | bytes 14000000 | tf_op jit(solution)/shard_map/feed/pallas_call | solution.py:501
  38.1 2.4 %all-gather.4 = bf16[800,512]{1,0:T(8,128)(2,1)S(1)} all-gather(bf16[400,512]{1,0:T(8,128)(2,1)S(1)} %get-tuple-element.43), channel_id=6, replica_groups=mesh['clip'=128,'mp'=2] {'mp'}, dimensions={0}, use_global_device_ids=true | all-gather | bytes 1228800 | tf_op jit(solution)/shard_map/all_gather | solution.py:576
  40.5 0.9 %finish.1 = (bf16[3,128,512]{2,1,0:T(8,128)(2,1)}, bf16[1,4,512]{2,1,0:T(4,128)(2,1)}) custom-call(f32[400,512]{1,0:T(8,128)S(1)} %get-tuple-element.42.base, bf16[2,400,512]{2,1,0:T(8,128)(2,1)S(1)} %bitcast.10), custom_call_target="tpu_custom_call" | custom-call | tf_op jit(solution)/shard_map/finish/pallas_call | solution.py:578
  (2 shorter events, 0.1 us)
Async XLA Ops:
  1.7 12.3 %collective-permute-start = (bf16[128,512]{1,0:T(8,128)(2,1)S(1)}, bf16[128,512]{1,0:T(8,128)(2,1)S(1)}, u32[]{:S(2)}, u32[]{:S(2)}) collective-permute-start(bf16[128,512]{1,0:T(8,128)(2,1)S(1)} %get-tuple-element.27), channel_id=1, source_target_pairs={{0,4},{2,6},{4,0},{6,2},{8,12},{10,14},{12,8},{14,10},{16,20},{18,... | collective-permute-start | bytes 393224 | tf_op jit(solution)/shard_map/ppermute | solution.py:33
  5.4 8.6 %collective-permute-start.1 = (bf16[128,512]{1,0:T(8,128)(2,1)S(1)}, bf16[128,512]{1,0:T(8,128)(2,1)S(1)}, u32[]{:S(2)}, u32[]{:S(2)}) collective-permute-start(bf16[128,512]{1,0:T(8,128)(2,1)S(1)} %get-tuple-element.28), channel_id=1, source_target_pairs={{0,2},{2,0},{4,6},{6,4},{8,10},{10,8},{12,14},{14,12},{16,18},{18,... | collective-permute-start | bytes 393224 | tf_op jit(solution)/shard_map/ppermute | solution.py:33
  5.7 8.3 %collective-permute-start.2 = (bf16[128,512]{1,0:T(8,128)(2,1)S(1)}, bf16[128,512]{1,0:T(8,128)(2,1)S(1)}, u32[]{:S(2)}, u32[]{:S(2)}) collective-permute-start(bf16[128,512]{1,0:T(8,128)(2,1)S(1)} %get-tuple-element.29), channel_id=1, source_target_pairs={{0,6},{2,4},{4,2},{6,0},{8,14},{10,12},{12,10},{14,8},{16,22},{18,... | collective-permute-start | bytes 393224 | tf_op jit(solution)/shard_map/ppermute | solution.py:33
  11.2 21.1 %collective-permute-start.6 = (bf16[512,1024]{1,0:T(8,128)(2,1)}, bf16[512,1024]{1,0:T(8,128)(2,1)S(1)}, u32[]{:S(2)}, u32[]{:S(2)}) collective-permute-start(bf16[512,1024]{1,0:T(8,128)(2,1)} %w_out.1), channel_id=1, source_target_pairs={{0,1},{1,0},{2,3},{3,2},{4,5},{5,4},{6,7},{7,6},{8,9},{9,8},{10,11... | collective-permute-start | bytes 3145736 | tf_op jit(solution)/shard_map/ppermute | solution.py:557
  16.4 15.9 %copy-start.2 = (bf16[2048,1024]{1,0:T(8,128)(2,1)S(1)}, bf16[2048,1024]{1,0:T(8,128)(2,1)}, u32[]{:S(2)}) copy-start(bf16[2048,1024]{1,0:T(8,128)(2,1)} %w_down.1) | copy-start | bytes 12582916
  19.3 13.0 %copy-start = (s32[128,3]{0,1:T(4,128)S(1)}, s32[128,3]{0,1:T(4,128)}, u32[]{:S(2)}) copy-start(s32[128,3]{0,1:T(4,128)} %param.15) | copy-start | bytes 4612
  19.3 13.0 %copy-start.1 = (bf16[1024,2048]{1,0:T(8,128)(2,1)S(1)}, bf16[1024,2048]{1,0:T(8,128)(2,1)}, u32[]{:S(2)}) copy-start(bf16[1024,2048]{1,0:T(8,128)(2,1)} %w_up.1) | copy-start | bytes 12582916
  19.3 13.0 %copy-start.3 = (bf16[512,1024]{1,0:T(8,128)(2,1)S(1)}, bf16[512,1024]{1,0:T(8,128)(2,1)}, u32[]{:S(2)}) copy-start(bf16[512,1024]{1,0:T(8,128)(2,1)} %w_out.1) | copy-start | bytes 3145732
  19.4 13.0 %copy-start.4 = (f32[1024]{0:T(1024)S(1)}, f32[1024]{0:T(1024)}, u32[]{:S(2)}) copy-start(f32[1024]{0:T(1024)} %param.19) | copy-start | bytes 12292
  19.4 7.3 %collective-permute-start.3 = (bf16[128,512]{1,0:T(8,128)(2,1)S(1)}, bf16[128,512]{1,0:T(8,128)(2,1)S(1)}, u32[]{:S(2)}, u32[]{:S(2)}) collective-permute-start(bf16[128,512]{1,0:T(8,128)(2,1)S(1)} %get-tuple-element.37), channel_id=1, source_target_pairs={{0,4},{2,6},{4,0},{6,2},{8,12},{10,14},{12,8},{14,10},{16,20},{18,... | collective-permute-start | bytes 393224 | tf_op jit(solution)/shard_map/ppermute | solution.py:33
  22.9 6.4 %collective-permute-start.4 = (bf16[128,512]{1,0:T(8,128)(2,1)S(1)}, bf16[128,512]{1,0:T(8,128)(2,1)S(1)}, u32[]{:S(2)}, u32[]{:S(2)}) collective-permute-start(bf16[128,512]{1,0:T(8,128)(2,1)S(1)} %near.1), channel_id=1, source_target_pairs={{0,2},{2,0},{4,6},{6,4},{8,10},{10,8},{12,14},{14,12},{16,18},{18,... | collective-permute-start | bytes 393224 | tf_op jit(solution)/shard_map/ppermute | solution.py:33
  23.0 6.3 %collective-permute-start.5 = (bf16[128,512]{1,0:T(8,128)(2,1)S(1)}, bf16[128,512]{1,0:T(8,128)(2,1)S(1)}, u32[]{:S(2)}, u32[]{:S(2)}) collective-permute-start(bf16[128,512]{1,0:T(8,128)(2,1)S(1)} %get-tuple-element.40), channel_id=1, source_target_pairs={{0,6},{2,4},{4,2},{6,0},{8,14},{10,12},{12,10},{14,8},{16,22},{18,... | collective-permute-start | bytes 393224 | tf_op jit(solution)/shard_map/ppermute | solution.py:33

commit v3 on v2

--- a/solution.py
+++ b/solution.py
@@ -152,57 +152,72 @@
 END = CLIP_ROWS + PAD
 
 
-def token_block(query, keys, values, context, place, block, first, count):
+def token_blocks(query, keys, values, context, targets, count):
     pairs = values.shape[0]
     low = lax.broadcasted_iota(jnp.int32, (BLK, BLK), 1) < HEAD_DIM
     real = lax.broadcasted_iota(jnp.int32, (PAD, 2 * BLK), 0) < NB
-    start = pl.multiple_of(first * BLK, BLK)
-    at = pl.multiple_of(block * BLK, BLK)
     seen = count * BLK
-    cols = [slice(p * BLK, (p + 1) * BLK) for p in range(pairs)]
+    chains = [(place, block, first, p) for p in range(pairs) for place, block, first in targets]
     scores = []
-    for p in range(pairs):
-        q = query[pl.ds(at, BLK), cols[p]]
+    for place, block, first, p in chains:
+        cols = slice(p * BLK, (p + 1) * BLK)
+        start = pl.multiple_of(first * BLK, BLK)
+        q = query[pl.ds(pl.multiple_of(block * BLK, BLK), BLK), cols]
         none = jnp.zeros_like(q)
         both = jnp.concatenate([jnp.where(low, q, none), jnp.where(low, none, q)], axis=0)
-        k = jnp.concatenate([keys[pl.ds(start, seen), cols[p]], keys[CLIP_ROWS:END, cols[p]]], axis=0)
+        k = jnp.concatenate([keys[pl.ds(start, seen), cols], keys[CLIP_ROWS:END, cols]], axis=0)
         s = lax.dot_general(k, both, NT, preferred_element_type=F32)
         scores.append((s[:seen], jnp.where(real, s[seen:], -1e30)))
-    tops = [
-        jnp.maximum(jnp.max(s, axis=0, keepdims=True), jnp.max(se, axis=0, keepdims=True))
-        for s, se in scores
-    ]
-    parts = [
-        jnp.concatenate([jnp.exp(s - top).astype(BF16), jnp.exp(se - top).astype(BF16)], axis=0)
-        for (s, se), top in zip(scores, tops)
-    ]
+    parts = []
+    for s, se in scores:
+        top = jnp.maximum(jnp.max(s, axis=0, keepdims=True), jnp.max(se, axis=0, keepdims=True))
+        parts.append(
+            jnp.concatenate([jnp.exp(s - top).astype(BF16), jnp.exp(se - top).astype(BF16)], axis=0)
+        )
     sums = []
-    for p in range(pairs):
+    for (place, block, first, p), part in zip(chains, parts):
+        start = pl.multiple_of(first * BLK, BLK)
         v = jnp.concatenate([values[p, :, pl.ds(start, seen)], values[p, :, CLIP_ROWS:END]], axis=1)
-        sums.append(jnp.dot(v, parts[p], preferred_element_type=F32))
-    for p in range(pairs):
-        o = sums[p]
+        sums.append(jnp.dot(v, part, preferred_element_type=F32))
+    for (place, block, first, p), o in zip(chains, sums):
         total = o[BLK : BLK + 1]
         o = jnp.concatenate(
             [o[:HEAD_DIM, :BLK] / total[:, :BLK], o[HEAD_DIM:BLK, BLK:] / total[:, BLK:]], axis=0
         )
-        context[place, :, cols[p]] = o.T.astype(BF16)
+        context[place, :, p * BLK : (p + 1) * BLK] = o.T.astype(BF16)
+
+
+def sight(info, place):
+    block = info[0, place]
+    length = info[0, GROUP]
+    video = info[0, GROUP + 1]
+    is_video = block < video
+    first = jnp.where(is_video, 0, video)
+    seen = jnp.where(is_video, video, length - video)
+    return block, first, jnp.where(block < 0, 0, seen)
 
 
 def visit_blocks(info, places, query, keys, values, context):
+    sights = [sight(info, place) for place in places]
+    if len(places) == 2:
+        alike = sights[0][2] == sights[1][2]
+        for count in range(1, SLOT_DEV):
+
+            @pl.when(alike & (sights[0][2] == count))
+            def _():
+                targets = [(i, block, first) for i, (block, first, _) in enumerate(sights)]
+                token_blocks(query, keys, values, context, targets, count)
+
+    else:
+        alike = False
+
     def visit(i, carry):
-        place = places[0] + i * (places[-1] - places[0])
-        block = info[0, place]
-        length = info[0, GROUP]
-        video = info[0, GROUP + 1]
-        is_video = block < video
-        first = jnp.where(is_video, 0, video)
-        seen = jnp.where(is_video, video, length - video)
+        block, first, seen = sight(info, places[0] + i * (places[-1] - places[0]))
         for count in range(1, SLOT_DEV):
 
-            @pl.when((block >= 0) & (seen == count))
+            @pl.when(jnp.logical_not(alike) & (seen == count))
             def _():
-                token_block(query, keys, values, context, i, block, first, count)
+                token_blocks(query, keys, values, context, [(i, block, first)], count)
 
         return carry
 
@@ -359,48 +374,39 @@
         at = jnp.where(step == STEPS[0], 0, jnp.where(step == STEPS[1], 1, 2))
         at = pl.multiple_of(at * BLK, BLK)
         rows = slice(s * BLK, (s + 1) * BLK)
-
-        @pl.when(step == 0)
-        def _():
-            for k in range(2):
-                context[k, rows, :] = own[sides[k], :BLK, :]
-
-        @pl.when(step > 0)
-        def _():
-            for k in range(2):
-                context[k, rows, :] = arrived[sides[k], pl.ds(at, BLK), :]
-
-        @pl.when(step < 0)
-        def _():
-            for k in range(2):
-                context[k, rows, :] = jnp.zeros((BLK, half), BF16)
-
+        mine = jnp.full((BLK, half), step, jnp.int32) == 0
+        for k in range(2):
+            context[k, rows, :] = jnp.where(
+                mine, own[sides[k], :BLK, :], arrived[sides[k], pl.ds(at, BLK), :]
+            )
     for k in range(2):
         context[k, STORED:, :] = own[sides[k], BLK:, :]
 
-    tile = 256
-    for j in range(0, 2 * half, tile):
-        got = jnp.dot(context[0], w_out[:, j : j + tile], preferred_element_type=F32)
-        got = got + jnp.dot(context[1], w_out_other[:, j : j + tile], preferred_element_type=F32)
-        side, off = divmod(j, half)
-        got = got + stored[side, :, off : off + tile].astype(F32)
-        after[:, j : j + tile] = got.astype(BF16)
+    tile = 512
     gains = gain[...]
-    for r in range(0, ROWS, 80):
-        norm_into(after[r : r + 80, :half], after[r : r + 80, half:], gains, normed, r, 80)
-    for j in range(0, hidden, tile):
-        got = jnp.dot(normed[...], w_up[:, j : j + tile], preferred_element_type=F32)
-        active[:, j : j + tile] = jax.nn.gelu(got, approximate=True).astype(BF16)
-    for j in range(0, half, tile):
-        other = pl.multiple_of((1 - core) * half + j, tile)
-        got = jnp.dot(active[...], w_down[:, pl.ds(other, tile)], preferred_element_type=F32)
-        for rows, keep in kept:
-            send[rows, j : j + tile] = jnp.where(keep, got[rows], 0.0).astype(BF16)
-        mine = pl.multiple_of(core * half + j, tile)
-        got = jnp.dot(active[...], w_down[:, pl.ds(mine, tile)], preferred_element_type=F32)
-        got = got + after[:, pl.ds(mine, tile)].astype(F32)
-        for rows, keep in kept:
-            base[rows, j : j + tile] = jnp.where(keep, got[rows], 0.0)
+    halves = (slice(0, 208), slice(208, ROWS))
+    for rows in halves:
+        for side in range(2):
+            cols = slice(side * half, (side + 1) * half)
+            got = jnp.dot(context[0, rows, :], w_out[:, cols], preferred_element_type=F32)
+            got = got + jnp.dot(context[1, rows, :], w_out_other[:, cols], preferred_element_type=F32)
+            after[rows, cols] = (got + stored[side, rows, :].astype(F32)).astype(BF16)
+    for rows in halves:
+        norm_into(
+            after[rows, :half], after[rows, half:], gains, normed, rows.start, rows.stop - rows.start
+        )
+        for j in range(0, hidden, tile):
+            got = jnp.dot(normed[rows, :], w_up[:, j : j + tile], preferred_element_type=F32)
+            active[rows, j : j + tile] = jax.nn.gelu(got, approximate=True).astype(BF16)
+    other = pl.multiple_of((1 - core) * half, half)
+    got = jnp.dot(active[...], w_down[:, pl.ds(other, half)], preferred_element_type=F32)
+    for rows, keep in kept:
+        send[rows, :] = jnp.where(keep, got[rows], 0.0).astype(BF16)
+    mine = pl.multiple_of(core * half, half)
+    got = jnp.dot(active[...], w_down[:, pl.ds(mine, half)], preferred_element_type=F32)
+    got = got + after[:, pl.ds(mine, half)].astype(F32)
+    for rows, keep in kept:
+        base[rows, :] = jnp.where(keep, got[rows], 0.0)
 
 
 def finish_kernel(base, sums, mixed, merged):

time: 41.7 us -> 41.2 us (0.988)
  Pallas kernels: 16.8 us -> 15.4 us
  starting transfers between devices: 8.46 us -> 9.29 us
    pallas_call x2, Pallas kernels: 3.74 us -> 2.57 us  [part(): pl.pallas_call(kernel, name=name, out_shape=spec((rows, width)), in_specs...]
    ppermute x6, starting transfers between devices: 8.08 us -> 8.92 us  [partner(): lax.ppermute(x, 'clip', [(i, i ^ step) for i in range(lax.axis_size('clip...]
  transfers between devices with their start and end apart: 7 -> 7, of which waited for: 0 -> 0; matrix products, arithmetic and copies ran while one was open for 0% -> 0% of each run, Pallas kernels for 22% -> 19%
where the time goes in v3:
time: 41.2 us
  blocking collectives  15.6 us (38%)
  Pallas kernels  15.4 us (37%)
  starting transfers between devices  9.29 us (23%)
  between operations  0.78 us (2%)
    ppermute x6, starting transfers between devices, partner(): lax.ppermute(x, 'clip', [(i, i ^ step) for i in range(lax.axis_size('clip...  8.92 us
    all_gather x2, blocking collectives, body(): lax.all_gather(jnp.concatenate([far, near, across], axis=0), 'mp', axis=0)  5.54 us
    pallas_call x1, Pallas kernels, feed(): pl.pallas_call(feed_kernel, name='feed', out_shape=(spec((ROWS, width), F...  5.52 us
    all_gather x1, blocking collectives, body(): stored_all = lax.all_gather(stored, 'mp', axis=0)  4.9 us
    pallas_call x1, Pallas kernels, attend(): pl.pallas_call(attend_kernel, name='attend', out_shape=(block, block, spe...  2.93 us
    all_gather x1, blocking collectives, body(): own_all = lax.all_gather(own, 'mp', axis=0)  2.76 us
    pallas_call x2, Pallas kernels, part(): pl.pallas_call(kernel, name=name, out_shape=spec((rows, width)), in_specs...  2.57 us
    pallas_call x1, Pallas kernels, ready(): pl.pallas_call(ready_kernel, name='ready', out_shape=(spec(w_qkv.shape),...  2.45 us
  transfers between devices with their start and end apart: 7, of which 0 were waited for; matrix products, arithmetic and copies ran while one was open for 0% of the time, Pallas kernels for 19%

profile of v3, /device:TPU:1, one launch (start us, length us, event | category | flops | bytes accessed | tf_op | source)
XLA Modules:
  0.0 41.2 jit_solution(14873713544646417789)
XLA Ops:
  0.6 1.1 %pack.1 = (bf16[128,512]{1,0:T(8,128)(2,1)S(1)}, bf16[128,512]{1,0:T(8,128)(2,1)S(1)}, bf16[128,512]{1,0:T(8,128)(2,1)S(1)}, bf16[400,512]{1,0:T(8,128)(2,1)S(1)}) custom-call(s32[3,128]{1,0:T(4,128)} %bitcast.14, bf16[3,128,512]{2,1,0:T(8,128)(2,1)} %tokens.1, bf16[1,4,512]{2,1,0:T(4,128)(2,1)} %extra.1), custom_call_target="tpu_custom_call" | custom-call | tf_op jit(solution)/shard_map/pack/pallas_call | solution.py:544
  1.7 3.7 %collective-permute-start = (bf16[128,512]{1,0:T(8,128)(2,1)S(1)}, bf16[128,512]{1,0:T(8,128)(2,1)S(1)}, u32[]{:S(2)}, u32[]{:S(2)}) collective-permute-start(bf16[128,512]{1,0:T(8,128)(2,1)S(1)} %get-tuple-element.27), channel_id=1, source_target_pairs={{0,4},{2,6},{4,0},{6,2},{8,12},{10,14},{12,8},{14,10},{16,20},{18,... | collective-permute-start | bytes 393224 | tf_op jit(solution)/shard_map/ppermute | solution.py:33
  5.4 0.3 collective-permute-start.1
  5.7 0.6 %collective-permute-start.2 = (bf16[128,512]{1,0:T(8,128)(2,1)S(1)}, bf16[128,512]{1,0:T(8,128)(2,1)S(1)}, u32[]{:S(2)}, u32[]{:S(2)}) collective-permute-start(bf16[128,512]{1,0:T(8,128)(2,1)S(1)} %get-tuple-element.29), channel_id=1, source_target_pairs={{0,6},{2,4},{4,2},{6,0},{8,14},{10,12},{12,10},{14,8},{16,22},{18,... | collective-permute-start | bytes 393224 | tf_op jit(solution)/shard_map/ppermute | solution.py:33
  6.3 4.9 %all-gather = bf16[800,512]{1,0:T(8,128)(2,1)S(1)} all-gather(bf16[400,512]{1,0:T(8,128)(2,1)S(1)} %get-tuple-element.23), channel_id=2, replica_groups=mesh['clip'=128,'mp'=2] {'mp'}, dimensions={0}, use_global_device_ids=true | all-gather | bytes 1228800 | tf_op jit(solution)/shard_map/all_gather | solution.py:561
  11.2 0.4 collective-permute-start.6
  11.5 2.4 %ready.1 = (bf16[3,1024,512]{2,1,0:T(8,128)(2,1)S(1)}, bf16[144,512]{1,0:T(8,128)(2,1)S(1)}, bf16[144,512]{1,0:T(8,128)(2,1)S(1)}, bf16[4,128,144]{2,1,0:T(8,128...) custom-call(s32[3,128]{1,0:T(4,128)} %bitcast.15, s32[128]{0:T(128)} %all_lengths.1, s32[128]{0:T(128)} %all_videos.1, ...), custom_call_target="tpu_custom_call" | custom-call | flops 450000000 | bytes 4000000 | tf_op jit(solution)/shard_map/ready/pallas_call | solution.py:430
  14.0 0.0 collective-permute-done
  14.0 0.0 collective-permute-done.1
  14.0 0.0 collective-permute-done.2
  14.1 2.4 %all-gather.1 = bf16[768,512]{1,0:T(8,128)(2,1)S(1)} all-gather(bf16[384,512]{1,0:T(8,128)(2,1)S(1)} %pad_maximum_fusion), channel_id=3, replica_groups=mesh['clip'=128,'mp'=2] {'mp'}, dimensions={0}, use_global_device_ids=true | all-gather | bytes 1179648 | tf_op jit(solution)/shard_map/all_gather | solution.py:567
  16.4 0.0 copy-start.2
  16.4 2.9 %attend.1 = (bf16[128,512]{1,0:T(8,128)(2,1)S(1)}, bf16[128,512]{1,0:T(8,128)(2,1)S(1)}, bf16[768,512]{1,0:T(8,128)(2,1)S(1)}, bf16[768,512]{1,0:T(8,128)(2,1)S(1)}, bf16[4,144,768]{2,1,0:T(8,128)(2,1)S(1)}) custom-call(s32[1,8]{1,0:T(1,128)S(1)} %get-tuple-element.25.facts, f32[1,1024]{1,0:T(1,128)S(1)} %get-tuple-element.26.gain, ...), custom_call_target="tpu_custom_call" | custom-call | flops 1800000000 | bytes 6000000 | tf_op jit(solution)/shard_map/attend/pallas_call | solution.py:462
  19.4 0.0 copy-start
  19.4 0.0 copy-start.1
  19.4 0.0 copy-start.3
  19.4 0.0 copy-start.4
  19.4 1.3 %collective-permute-start.3 = (bf16[128,512]{1,0:T(8,128)(2,1)S(1)}, bf16[128,512]{1,0:T(8,128)(2,1)S(1)}, u32[]{:S(2)}, u32[]{:S(2)}) collective-permute-start(bf16[128,512]{1,0:T(8,128)(2,1)S(1)} %get-tuple-element.37), channel_id=1, source_target_pairs={{0,4},{2,6},{4,0},{6,2},{8,12},{10,14},{12,8},{14,10},{16,20},{18,... | collective-permute-start | bytes 393224 | tf_op jit(solution)/shard_map/ppermute | solution.py:33
  20.7 0.6 %near.1 = bf16[128,512]{1,0:T(8,128)(2,1)S(1)} custom-call(bf16[768,512]{1,0:T(8,128)(2,1)S(1)} %get-tuple-element.34.query, bf16[768,512]{1,0:T(8,128)(2,1)S(1)} %get-tuple-element.35.keys, bf16[4,144,768]{2,1,0:T(8,128)(2,1)S(1)} %get-tuple-element.36.values, s32[1,8]{1,0:T(1,128)S(1)} %get-tuple-element.25.facts), custom_call_target="tpu_custom_call" | custom-call | flops 400000000 | bytes 3000000 | tf_op jit(solution)/shard_map/near/pallas_call | solution.py:487
  21.3 2.0 %collective-permute-start.4 = (bf16[128,512]{1,0:T(8,128)(2,1)S(1)}, bf16[128,512]{1,0:T(8,128)(2,1)S(1)}, u32[]{:S(2)}, u32[]{:S(2)}) collective-permute-start(bf16[128,512]{1,0:T(8,128)(2,1)S(1)} %near.1), channel_id=1, source_target_pairs={{0,2},{2,0},{4,6},{6,4},{8,10},{10,8},{12,14},{14,12},{16,18},{18,... | collective-permute-start | bytes 393224 | tf_op jit(solution)/shard_map/ppermute | solution.py:33
  23.2 1.2 %collective-permute-start.5 = (bf16[128,512]{1,0:T(8,128)(2,1)S(1)}, bf16[128,512]{1,0:T(8,128)(2,1)S(1)}, u32[]{:S(2)}, u32[]{:S(2)}) collective-permute-start(bf16[128,512]{1,0:T(8,128)(2,1)S(1)} %get-tuple-element.40), channel_id=1, source_target_pairs={{0,6},{2,4},{4,2},{6,0},{8,14},{10,12},{12,10},{14,8},{16,22},{18,... | collective-permute-start | bytes 393224 | tf_op jit(solution)/shard_map/ppermute | solution.py:33
  24.4 2.0 %own.1 = bf16[144,512]{1,0:T(8,128)(2,1)S(1)} custom-call(bf16[768,512]{1,0:T(8,128)(2,1)S(1)} %get-tuple-element.34.query, bf16[768,512]{1,0:T(8,128)(2,1)S(1)} %get-tuple-element.35.keys, bf16[4,144,768]{2,1,0:T(8,128)(2,1)S(1)} %get-tuple-element.36.values, s32[1,8]{1,0:T(1,128)S(1)} %get-tuple-element.25.facts), custom_call_target="tpu_custom_call" | custom-call | flops 400000000 | bytes 3000000 | tf_op jit(solution)/shard_map/own/pallas_call | solution.py:487
  26.4 0.0 collective-permute-done.3
  26.4 2.8 %all-gather.2 = bf16[288,512]{1,0:T(8,128)(2,1)S(1)} all-gather(bf16[144,512]{1,0:T(8,128)(2,1)S(1)} %own.1), channel_id=4, replica_groups=mesh['clip'=128,'mp'=2] {'mp'}, dimensions={0}, use_global_device_ids=true | all-gather | bytes 442368 | tf_op jit(solution)/shard_map/all_gather | solution.py:576
  29.2 0.0 collective-permute-done.4
  29.2 0.0 collective-permute-done.5
  29.2 3.2 %all-gather.3 = bf16[768,512]{1,0:T(8,128)(2,1)S(1)} all-gather(bf16[384,512]{1,0:T(8,128)(2,1)S(1)} %pad_maximum_fusion.1), channel_id=5, replica_groups=mesh['clip'=128,'mp'=2] {'mp'}, dimensions={0}, use_global_device_ids=true | all-gather | bytes 1179648 | tf_op jit(solution)/shard_map/all_gather | solution.py:577
  32.4 0.0 collective-permute-done.6.w_out_other
  32.4 0.0 copy-done.2
  32.4 0.0 copy-done
  32.4 0.0 copy-done.1
  32.4 0.0 copy-done.3
  32.4 0.0 copy-done.4
  32.4 5.5 %feed.1 = (f32[400,512]{1,0:T(8,128)S(1)}, bf16[400,512]{1,0:T(8,128)(2,1)S(1)}) custom-call(s32[3,128]{1,0:T(4,128)S(1)} %bitcast.16, bf16[2,400,512]{2,1,0:T(8,128)(2,1)S(1)} %bitcast.9, bf16[2,144,512]{2,1,0:T(8,128)(2,1)S(1)} %bitcast.13, bf16[2,384,512]{2,1,0:T(8,128)(2,1)S(1)} %bitcast.12, bf16[512,1024]{1,0:T(8,128)(2,1)S(1)} %copy-done.3, ...), custom_call_target="tpu_custom_call" | custom-call | flops 4100000000 | bytes 14000000 | tf_op jit(solution)/shard_map/feed/pallas_call | solution.py:507
  37.9 2.4 %all-gather.4 = bf16[800,512]{1,0:T(8,128)(2,1)S(1)} all-gather(bf16[400,512]{1,0:T(8,128)(2,1)S(1)} %get-tuple-element.43), channel_id=6, replica_groups=mesh['clip'=128,'mp'=2] {'mp'}, dimensions={0}, use_global_device_ids=true | all-gather | bytes 1228800 | tf_op jit(solution)/shard_map/all_gather | solution.py:582
  40.3 0.9 %finish.1 = (bf16[3,128,512]{2,1,0:T(8,128)(2,1)}, bf16[1,4,512]{2,1,0:T(4,128)(2,1)}) custom-call(f32[400,512]{1,0:T(8,128)S(1)} %get-tuple-element.42.base, bf16[2,400,512]{2,1,0:T(8,128)(2,1)S(1)} %bitcast.10), custom_call_target="tpu_custom_call" | custom-call | tf_op jit(solution)/shard_map/finish/pallas_call | solution.py:584
  (2 shorter events, 0.1 us)
Async XLA Ops:
  1.7 12.3 %collective-permute-start = (bf16[128,512]{1,0:T(8,128)(2,1)S(1)}, bf16[128,512]{1,0:T(8,128)(2,1)S(1)}, u32[]{:S(2)}, u32[]{:S(2)}) collective-permute-start(bf16[128,512]{1,0:T(8,128)(2,1)S(1)} %get-tuple-element.27), channel_id=1, source_target_pairs={{0,4},{2,6},{4,0},{6,2},{8,12},{10,14},{12,8},{14,10},{16,20},{18,... | collective-permute-start | bytes 393224 | tf_op jit(solution)/shard_map/ppermute | solution.py:33
  5.4 8.6 %collective-permute-start.1 = (bf16[128,512]{1,0:T(8,128)(2,1)S(1)}, bf16[128,512]{1,0:T(8,128)(2,1)S(1)}, u32[]{:S(2)}, u32[]{:S(2)}) collective-permute-start(bf16[128,512]{1,0:T(8,128)(2,1)S(1)} %get-tuple-element.28), channel_id=1, source_target_pairs={{0,2},{2,0},{4,6},{6,4},{8,10},{10,8},{12,14},{14,12},{16,18},{18,... | collective-permute-start | bytes 393224 | tf_op jit(solution)/shard_map/ppermute | solution.py:33
  5.7 8.3 %collective-permute-start.2 = (bf16[128,512]{1,0:T(8,128)(2,1)S(1)}, bf16[128,512]{1,0:T(8,128)(2,1)S(1)}, u32[]{:S(2)}, u32[]{:S(2)}) collective-permute-start(bf16[128,512]{1,0:T(8,128)(2,1)S(1)} %get-tuple-element.29), channel_id=1, source_target_pairs={{0,6},{2,4},{4,2},{6,0},{8,14},{10,12},{12,10},{14,8},{16,22},{18,... | collective-permute-start | bytes 393224 | tf_op jit(solution)/shard_map/ppermute | solution.py:33
  11.2 21.2 %collective-permute-start.6 = (bf16[512,1024]{1,0:T(8,128)(2,1)}, bf16[512,1024]{1,0:T(8,128)(2,1)S(1)}, u32[]{:S(2)}, u32[]{:S(2)}) collective-permute-start(bf16[512,1024]{1,0:T(8,128)(2,1)} %w_out.1), channel_id=1, source_target_pairs={{0,1},{1,0},{2,3},{3,2},{4,5},{5,4},{6,7},{7,6},{8,9},{9,8},{10,11... | collective-permute-start | bytes 3145736 | tf_op jit(solution)/shard_map/ppermute | solution.py:563
  16.4 16.0 %copy-start.2 = (bf16[2048,1024]{1,0:T(8,128)(2,1)S(1)}, bf16[2048,1024]{1,0:T(8,128)(2,1)}, u32[]{:S(2)}) copy-start(bf16[2048,1024]{1,0:T(8,128)(2,1)} %w_down.1) | copy-start | bytes 12582916
  19.4 13.0 %copy-start = (s32[128,3]{0,1:T(4,128)S(1)}, s32[128,3]{0,1:T(4,128)}, u32[]{:S(2)}) copy-start(s32[128,3]{0,1:T(4,128)} %param.15) | copy-start | bytes 4612
  19.4 13.0 %copy-start.1 = (bf16[1024,2048]{1,0:T(8,128)(2,1)S(1)}, bf16[1024,2048]{1,0:T(8,128)(2,1)}, u32[]{:S(2)}) copy-start(bf16[1024,2048]{1,0:T(8,128)(2,1)} %w_up.1) | copy-start | bytes 12582916
  19.4 13.0 %copy-start.3 = (bf16[512,1024]{1,0:T(8,128)(2,1)S(1)}, bf16[512,1024]{1,0:T(8,128)(2,1)}, u32[]{:S(2)}) copy-start(bf16[512,1024]{1,0:T(8,128)(2,1)} %w_out.1) | copy-start | bytes 3145732
  19.4 13.0 %copy-start.4 = (f32[1024]{0:T(1024)S(1)}, f32[1024]{0:T(1024)}, u32[]{:S(2)}) copy-start(f32[1024]{0:T(1024)} %param.19) | copy-start | bytes 12292
  19.4 7.0 %collective-permute-start.3 = (bf16[128,512]{1,0:T(8,128)(2,1)S(1)}, bf16[128,512]{1,0:T(8,128)(2,1)S(1)}, u32[]{:S(2)}, u32[]{:S(2)}) collective-permute-start(bf16[128,512]{1,0:T(8,128)(2,1)S(1)} %get-tuple-element.37), channel_id=1, source_target_pairs={{0,4},{2,6},{4,0},{6,2},{8,12},{10,14},{12,8},{14,10},{16,20},{18,... | collective-permute-start | bytes 393224 | tf_op jit(solution)/shard_map/ppermute | solution.py:33
  21.3 7.9 %collective-permute-start.4 = (bf16[128,512]{1,0:T(8,128)(2,1)S(1)}, bf16[128,512]{1,0:T(8,128)(2,1)S(1)}, u32[]{:S(2)}, u32[]{:S(2)}) collective-permute-start(bf16[128,512]{1,0:T(8,128)(2,1)S(1)} %near.1), channel_id=1, source_target_pairs={{0,2},{2,0},{4,6},{6,4},{8,10},{10,8},{12,14},{14,12},{16,18},{18,... | collective-permute-start | bytes 393224 | tf_op jit(solution)/shard_map/ppermute | solution.py:33
  23.2 5.9 %collective-permute-start.5 = (bf16[128,512]{1,0:T(8,128)(2,1)S(1)}, bf16[128,512]{1,0:T(8,128)(2,1)S(1)}, u32[]{:S(2)}, u32[]{:S(2)}) collective-permute-start(bf16[128,512]{1,0:T(8,128)(2,1)S(1)} %get-tuple-element.40), channel_id=1, source_target_pairs={{0,6},{2,4},{4,2},{6,0},{8,14},{10,12},{12,10},{14,8},{16,22},{18,... | collective-permute-start | bytes 393224 | tf_op jit(solution)/shard_map/ppermute | solution.py:33

commit v4 on v3

--- a/solution.py
+++ b/solution.py
@@ -572,7 +572,7 @@
     near = part(near_kernel, "near", BLK, query, keys, values, facts)
     near = partner(near, 1)
     own = part(own_kernel, "own", BLK + PAD, query, keys, values, facts)
-    own, far = lax.optimization_barrier((own, far))
+    own, far, across = lax.optimization_barrier((own, far, across))
     own_all = lax.all_gather(own, "mp", axis=0)
     arrived = lax.all_gather(jnp.concatenate([far, near, across], axis=0), "mp", axis=0)
 

time: 41.2 us -> 43.3 us (1.051); the launches traced: 41.2 us -> 42.8 us
  waiting for transfers between devices: 0.02 us -> 3.45 us
  starting transfers between devices: 9.29 us -> 7.72 us
  blocking collectives: 15.6 us -> 14.2 us
  Pallas kernels: 15.4 us -> 16.6 us
    ppermute x6, waiting for transfers between devices: 0.02 us -> 3.45 us  [partner(): lax.ppermute(x, 'clip', [(i, i ^ step) for i in range(lax.axis_size('clip...]
    ppermute x6, starting transfers between devices: 8.92 us -> 7.34 us  [partner(): lax.ppermute(x, 'clip', [(i, i ^ step) for i in range(lax.axis_size('clip...]
    pallas_call x2, Pallas kernels: 2.57 us -> 3.54 us  [part(): pl.pallas_call(kernel, name=name, out_shape=spec((rows, width)), in_specs...]
    all_gather x2, blocking collectives: 5.54 us -> 4.74 us  [body(): lax.all_gather(jnp.concatenate([far, near, across], axis=0), 'mp', axis=0)]
    all_gather x1, blocking collectives: 2.76 us -> 2.13 us  [body(): own_all = lax.all_gather(own, 'mp', axis=0)]
  transfers between devices with their start and end apart: 7 -> 7, of which waited for: 0 -> 2; matrix products, arithmetic and copies ran while one was open for 0% -> 0% of each run, Pallas kernels for 19% -> 21%
where the time goes in v4:
time: 43.3 us; the launch traced here: 42.8 us
  Pallas kernels  16.6 us (38%)
  blocking collectives  14.2 us (33%)
  starting transfers between devices  7.72 us (18%)
  waiting for transfers between devices  3.45 us (8%)
  between operations  0.78 us (2%)
    ppermute x6, starting transfers between devices, partner(): lax.ppermute(x, 'clip', [(i, i ^ step) for i in range(lax.axis_size('clip...  7.34 us
    pallas_call x1, Pallas kernels, feed(): pl.pallas_call(feed_kernel, name='feed', out_shape=(spec((ROWS, width), F...  5.54 us
    all_gather x1, blocking collectives, body(): stored_all = lax.all_gather(stored, 'mp', axis=0)  4.9 us
    all_gather x2, blocking collectives, body(): lax.all_gather(jnp.concatenate([far, near, across], axis=0), 'mp', axis=0)  4.74 us
    pallas_call x2, Pallas kernels, part(): pl.pallas_call(kernel, name=name, out_shape=spec((rows, width)), in_specs...  3.54 us
    ppermute x6, waiting for transfers between devices, partner(): lax.ppermute(x, 'clip', [(i, i ^ step) for i in range(lax.axis_size('clip...  3.45 us
    pallas_call x1, Pallas kernels, attend(): pl.pallas_call(attend_kernel, name='attend', out_shape=(block, block, spe...  3.11 us
    pallas_call x1, Pallas kernels, ready(): pl.pallas_call(ready_kernel, name='ready', out_shape=(spec(w_qkv.shape),...  2.45 us
  transfers between devices with their start and end apart: 7, of which 2 were waited for; matrix products, arithmetic and copies ran while one was open for 0% of the time, Pallas kernels for 21%

profile of v4, /device:TPU:1, one launch (start us, length us, event | category | flops | bytes accessed | tf_op | source)
XLA Modules:
  0.0 42.8 jit_solution(14984177353444725217)
XLA Ops:
  0.6 1.1 %pack.1 = (bf16[128,512]{1,0:T(8,128)(2,1)S(1)}, bf16[128,512]{1,0:T(8,128)(2,1)S(1)}, bf16[128,512]{1,0:T(8,128)(2,1)S(1)}, bf16[400,512]{1,0:T(8,128)(2,1)S(1)}) custom-call(s32[3,128]{1,0:T(4,128)} %bitcast.14, bf16[3,128,512]{2,1,0:T(8,128)(2,1)} %tokens.1, bf16[1,4,512]{2,1,0:T(4,128)(2,1)} %extra.1), custom_call_target="tpu_custom_call" | custom-call | tf_op jit(solution)/shard_map/pack/pallas_call | solution.py:544
  1.7 3.7 %collective-permute-start = (bf16[128,512]{1,0:T(8,128)(2,1)S(1)}, bf16[128,512]{1,0:T(8,128)(2,1)S(1)}, u32[]{:S(2)}, u32[]{:S(2)}) collective-permute-start(bf16[128,512]{1,0:T(8,128)(2,1)S(1)} %get-tuple-element.28), channel_id=1, source_target_pairs={{0,4},{2,6},{4,0},{6,2},{8,12},{10,14},{12,8},{14,10},{16,20},{18,... | collective-permute-start | bytes 393224 | tf_op jit(solution)/shard_map/ppermute | solution.py:33
  5.4 0.3 collective-permute-start.1
  5.7 0.6 %collective-permute-start.2 = (bf16[128,512]{1,0:T(8,128)(2,1)S(1)}, bf16[128,512]{1,0:T(8,128)(2,1)S(1)}, u32[]{:S(2)}, u32[]{:S(2)}) collective-permute-start(bf16[128,512]{1,0:T(8,128)(2,1)S(1)} %get-tuple-element.30), channel_id=1, source_target_pairs={{0,6},{2,4},{4,2},{6,0},{8,14},{10,12},{12,10},{14,8},{16,22},{18,... | collective-permute-start | bytes 393224 | tf_op jit(solution)/shard_map/ppermute | solution.py:33
  6.3 4.9 %all-gather = bf16[800,512]{1,0:T(8,128)(2,1)S(1)} all-gather(bf16[400,512]{1,0:T(8,128)(2,1)S(1)} %get-tuple-element.24), channel_id=2, replica_groups=mesh['clip'=128,'mp'=2] {'mp'}, dimensions={0}, use_global_device_ids=true | all-gather | bytes 1228800 | tf_op jit(solution)/shard_map/all_gather | solution.py:561
  11.2 0.4 collective-permute-start.6
  11.5 2.4 %ready.1 = (bf16[3,1024,512]{2,1,0:T(8,128)(2,1)S(1)}, bf16[144,512]{1,0:T(8,128)(2,1)S(1)}, bf16[144,512]{1,0:T(8,128)(2,1)S(1)}, bf16[4,128,144]{2,1,0:T(8,128...) custom-call(s32[3,128]{1,0:T(4,128)} %bitcast.15, s32[128]{0:T(128)} %all_lengths.1, s32[128]{0:T(128)} %all_videos.1, ...), custom_call_target="tpu_custom_call" | custom-call | flops 450000000 | bytes 4000000 | tf_op jit(solution)/shard_map/ready/pallas_call | solution.py:430
  14.0 0.0 collective-permute-done
  14.0 0.0 collective-permute-done.1
  14.0 0.0 collective-permute-done.2
  14.1 2.4 %all-gather.1 = bf16[768,512]{1,0:T(8,128)(2,1)S(1)} all-gather(bf16[384,512]{1,0:T(8,128)(2,1)S(1)} %pad_maximum_fusion), channel_id=3, replica_groups=mesh['clip'=128,'mp'=2] {'mp'}, dimensions={0}, use_global_device_ids=true | all-gather | bytes 1179648 | tf_op jit(solution)/shard_map/all_gather | solution.py:567
  16.4 0.0 copy-start.2
  16.4 3.1 %attend.1 = (bf16[128,512]{1,0:T(8,128)(2,1)S(1)}, bf16[128,512]{1,0:T(8,128)(2,1)S(1)}, bf16[768,512]{1,0:T(8,128)(2,1)S(1)}, bf16[768,512]{1,0:T(8,128)(2,1)S(1)}, bf16[4,144,768]{2,1,0:T(8,128)(2,1)S(1)}) custom-call(s32[1,8]{1,0:T(1,128)S(1)} %get-tuple-element.26.facts, f32[1,1024]{1,0:T(1,128)S(1)} %get-tuple-element.27.gain, ...), custom_call_target="tpu_custom_call" | custom-call | flops 1800000000 | bytes 6000000 | tf_op jit(solution)/shard_map/attend/pallas_call | solution.py:462
  19.5 0.0 copy-start
  19.6 0.0 copy-start.1
  19.6 0.0 copy-start.3
  19.6 0.0 copy-start.4
  19.6 2.0 %collective-permute-start.3 = (bf16[128,512]{1,0:T(8,128)(2,1)S(1)}, bf16[128,512]{1,0:T(8,128)(2,1)S(1)}, u32[]{:S(2)}, u32[]{:S(2)}) collective-permute-start(bf16[128,512]{1,0:T(8,128)(2,1)S(1)} %get-tuple-element.38), channel_id=1, source_target_pairs={{0,4},{2,6},{4,0},{6,2},{8,12},{10,14},{12,8},{14,10},{16,20},{18,... | collective-permute-start | bytes 393224 | tf_op jit(solution)/shard_map/ppermute | solution.py:33
  21.6 0.0 collective-permute-start.4
  21.6 1.3 %near.1 = bf16[128,512]{1,0:T(8,128)(2,1)S(1)} custom-call(bf16[768,512]{1,0:T(8,128)(2,1)S(1)} %get-tuple-element.35.query, bf16[768,512]{1,0:T(8,128)(2,1)S(1)} %get-tuple-element.36.keys, bf16[4,144,768]{2,1,0:T(8,128)(2,1)S(1)} %get-tuple-element.37.values, s32[1,8]{1,0:T(1,128)S(1)} %get-tuple-element.26.facts), custom_call_target="tpu_custom_call" | custom-call | flops 400000000 | bytes 3000000 | tf_op jit(solution)/shard_map/near/pallas_call | solution.py:487
  23.0 0.8 %collective-permute-start.5 = (bf16[128,512]{1,0:T(8,128)(2,1)S(1)}, bf16[128,512]{1,0:T(8,128)(2,1)S(1)}, u32[]{:S(2)}, u32[]{:S(2)}) collective-permute-start(bf16[128,512]{1,0:T(8,128)(2,1)S(1)} %near.1), channel_id=1, source_target_pairs={{0,2},{2,0},{4,6},{6,4},{8,10},{10,8},{12,14},{14,12},{16,18},{18,... | collective-permute-start | bytes 393224 | tf_op jit(solution)/shard_map/ppermute | solution.py:33
  23.8 2.2 %own.1 = bf16[144,512]{1,0:T(8,128)(2,1)S(1)} custom-call(bf16[768,512]{1,0:T(8,128)(2,1)S(1)} %get-tuple-element.35.query, bf16[768,512]{1,0:T(8,128)(2,1)S(1)} %get-tuple-element.36.keys, bf16[4,144,768]{2,1,0:T(8,128)(2,1)S(1)} %get-tuple-element.37.values, s32[1,8]{1,0:T(1,128)S(1)} %get-tuple-element.26.facts), custom_call_target="tpu_custom_call" | custom-call | flops 400000000 | bytes 3000000 | tf_op jit(solution)/shard_map/own/pallas_call | solution.py:487
  26.0 0.1 collective-permute-done.3
  26.1 3.3 %collective-permute-done.4 = bf16[128,512]{1,0:T(8,128)(2,1)S(1)} collective-permute-done((bf16[128,512]{1,0:T(8,128)(2,1)S(1)}, bf16[128,512]{1,0:T(8,128)(2,1)S(1)}, u32[]{:S(2)}, u32[]{:S(2)}) %collective-permute-start.4) | collective-permute-done | bytes 131104 | tf_op jit(solution)/shard_map/ppermute | solution.py:33
  29.4 2.1 %all-gather.2 = bf16[288,512]{1,0:T(8,128)(2,1)S(1)} all-gather(bf16[144,512]{1,0:T(8,128)(2,1)S(1)} %own.1), channel_id=4, replica_groups=mesh['clip'=128,'mp'=2] {'mp'}, dimensions={0}, use_global_device_ids=true | all-gather | bytes 442368 | tf_op jit(solution)/shard_map/all_gather | solution.py:576
  31.5 0.0 collective-permute-done.5
  31.6 2.4 %all-gather.3 = bf16[768,512]{1,0:T(8,128)(2,1)S(1)} all-gather(bf16[384,512]{1,0:T(8,128)(2,1)S(1)} %pad_maximum_fusion.1), channel_id=5, replica_groups=mesh['clip'=128,'mp'=2] {'mp'}, dimensions={0}, use_global_device_ids=true | all-gather | bytes 1179648 | tf_op jit(solution)/shard_map/all_gather | solution.py:577
  33.9 0.0 collective-permute-done.6.w_out_other
  34.0 0.0 copy-done.2
  34.0 0.0 copy-done
  34.0 0.0 copy-done.1
  34.0 0.0 copy-done.3
  34.0 0.0 copy-done.4
  34.0 5.5 %feed.1 = (f32[400,512]{1,0:T(8,128)S(1)}, bf16[400,512]{1,0:T(8,128)(2,1)S(1)}) custom-call(s32[3,128]{1,0:T(4,128)S(1)} %bitcast.16, bf16[2,400,512]{2,1,0:T(8,128)(2,1)S(1)} %bitcast.9, bf16[2,144,512]{2,1,0:T(8,128)(2,1)S(1)} %bitcast.13, bf16[2,384,512]{2,1,0:T(8,128)(2,1)S(1)} %bitcast.12, bf16[512,1024]{1,0:T(8,128)(2,1)S(1)} %copy-done.3, ...), custom_call_target="tpu_custom_call" | custom-call | flops 4100000000 | bytes 14000000 | tf_op jit(solution)/shard_map/feed/pallas_call | solution.py:507
  39.5 2.4 %all-gather.4 = bf16[800,512]{1,0:T(8,128)(2,1)S(1)} all-gather(bf16[400,512]{1,0:T(8,128)(2,1)S(1)} %get-tuple-element.45), channel_id=6, replica_groups=mesh['clip'=128,'mp'=2] {'mp'}, dimensions={0}, use_global_device_ids=true | all-gather | bytes 1228800 | tf_op jit(solution)/shard_map/all_gather | solution.py:582
  41.9 0.9 %finish.1 = (bf16[3,128,512]{2,1,0:T(8,128)(2,1)}, bf16[1,4,512]{2,1,0:T(4,128)(2,1)}) custom-call(f32[400,512]{1,0:T(8,128)S(1)} %get-tuple-element.44.base, bf16[2,400,512]{2,1,0:T(8,128)(2,1)S(1)} %bitcast.10), custom_call_target="tpu_custom_call" | custom-call | tf_op jit(solution)/shard_map/finish/pallas_call | solution.py:584
  (2 shorter events, 0.1 us)
Async XLA Ops:
  1.7 12.3 %collective-permute-start = (bf16[128,512]{1,0:T(8,128)(2,1)S(1)}, bf16[128,512]{1,0:T(8,128)(2,1)S(1)}, u32[]{:S(2)}, u32[]{:S(2)}) collective-permute-start(bf16[128,512]{1,0:T(8,128)(2,1)S(1)} %get-tuple-element.28), channel_id=1, source_target_pairs={{0,4},{2,6},{4,0},{6,2},{8,12},{10,14},{12,8},{14,10},{16,20},{18,... | collective-permute-start | bytes 393224 | tf_op jit(solution)/shard_map/ppermute | solution.py:33
  5.4 8.6 %collective-permute-start.1 = (bf16[128,512]{1,0:T(8,128)(2,1)S(1)}, bf16[128,512]{1,0:T(8,128)(2,1)S(1)}, u32[]{:S(2)}, u32[]{:S(2)}) collective-permute-start(bf16[128,512]{1,0:T(8,128)(2,1)S(1)} %get-tuple-element.29), channel_id=1, source_target_pairs={{0,2},{2,0},{4,6},{6,4},{8,10},{10,8},{12,14},{14,12},{16,18},{18,... | collective-permute-start | bytes 393224 | tf_op jit(solution)/shard_map/ppermute | solution.py:33
  5.7 8.3 %collective-permute-start.2 = (bf16[128,512]{1,0:T(8,128)(2,1)S(1)}, bf16[128,512]{1,0:T(8,128)(2,1)S(1)}, u32[]{:S(2)}, u32[]{:S(2)}) collective-permute-start(bf16[128,512]{1,0:T(8,128)(2,1)S(1)} %get-tuple-element.30), channel_id=1, source_target_pairs={{0,6},{2,4},{4,2},{6,0},{8,14},{10,12},{12,10},{14,8},{16,22},{18,... | collective-permute-start | bytes 393224 | tf_op jit(solution)/shard_map/ppermute | solution.py:33
  11.2 22.8 %collective-permute-start.6 = (bf16[512,1024]{1,0:T(8,128)(2,1)}, bf16[512,1024]{1,0:T(8,128)(2,1)S(1)}, u32[]{:S(2)}, u32[]{:S(2)}) collective-permute-start(bf16[512,1024]{1,0:T(8,128)(2,1)} %w_out.1), channel_id=1, source_target_pairs={{0,1},{1,0},{2,3},{3,2},{4,5},{5,4},{6,7},{7,6},{8,9},{9,8},{10,11... | collective-permute-start | bytes 3145736 | tf_op jit(solution)/shard_map/ppermute | solution.py:563
  16.4 17.5 %copy-start.2 = (bf16[2048,1024]{1,0:T(8,128)(2,1)S(1)}, bf16[2048,1024]{1,0:T(8,128)(2,1)}, u32[]{:S(2)}) copy-start(bf16[2048,1024]{1,0:T(8,128)(2,1)} %w_down.1) | copy-start | bytes 12582916
  19.5 14.4 %copy-start = (s32[128,3]{0,1:T(4,128)S(1)}, s32[128,3]{0,1:T(4,128)}, u32[]{:S(2)}) copy-start(s32[128,3]{0,1:T(4,128)} %param.15) | copy-start | bytes 4612
  19.6 14.4 %copy-start.1 = (bf16[1024,2048]{1,0:T(8,128)(2,1)S(1)}, bf16[1024,2048]{1,0:T(8,128)(2,1)}, u32[]{:S(2)}) copy-start(bf16[1024,2048]{1,0:T(8,128)(2,1)} %w_up.1) | copy-start | bytes 12582916
  19.6 14.4 %copy-start.3 = (bf16[512,1024]{1,0:T(8,128)(2,1)S(1)}, bf16[512,1024]{1,0:T(8,128)(2,1)}, u32[]{:S(2)}) copy-start(bf16[512,1024]{1,0:T(8,128)(2,1)} %w_out.1) | copy-start | bytes 3145732
  19.6 14.4 %copy-start.4 = (f32[1024]{0:T(1024)S(1)}, f32[1024]{0:T(1024)}, u32[]{:S(2)}) copy-start(f32[1024]{0:T(1024)} %param.19) | copy-start | bytes 12292
  19.6 6.5 %collective-permute-start.3 = (bf16[128,512]{1,0:T(8,128)(2,1)S(1)}, bf16[128,512]{1,0:T(8,128)(2,1)S(1)}, u32[]{:S(2)}, u32[]{:S(2)}) collective-permute-start(bf16[128,512]{1,0:T(8,128)(2,1)S(1)} %get-tuple-element.38), channel_id=1, source_target_pairs={{0,4},{2,6},{4,0},{6,2},{8,12},{10,14},{12,8},{14,10},{16,20},{18,... | collective-permute-start | bytes 393224 | tf_op jit(solution)/shard_map/ppermute | solution.py:33
  21.6 7.8 %collective-permute-start.4 = (bf16[128,512]{1,0:T(8,128)(2,1)S(1)}, bf16[128,512]{1,0:T(8,128)(2,1)S(1)}, u32[]{:S(2)}, u32[]{:S(2)}) collective-permute-start(bf16[128,512]{1,0:T(8,128)(2,1)S(1)} %get-tuple-element.39), channel_id=1, source_target_pairs={{0,6},{2,4},{4,2},{6,0},{8,14},{10,12},{12,10},{14,8},{16,22},{18,... | collective-permute-start | bytes 393224 | tf_op jit(solution)/shard_map/ppermute | solution.py:33
  23.0 8.6 %collective-permute-start.5 = (bf16[128,512]{1,0:T(8,128)(2,1)S(1)}, bf16[128,512]{1,0:T(8,128)(2,1)S(1)}, u32[]{:S(2)}, u32[]{:S(2)}) collective-permute-start(bf16[128,512]{1,0:T(8,128)(2,1)S(1)} %near.1), channel_id=1, source_target_pairs={{0,2},{2,0},{4,6},{6,4},{8,10},{10,8},{12,14},{14,12},{16,18},{18,... | collective-permute-start | bytes 393224 | tf_op jit(solution)/shard_map/ppermute | solution.py:33

commit v5 on v3

--- a/solution.py
+++ b/solution.py
@@ -1,3 +1,5 @@
+import itertools
+
 import jax
 import jax.numpy as jnp
 from jax import lax
@@ -152,16 +154,18 @@
 END = CLIP_ROWS + PAD
 
 
-def token_blocks(query, keys, values, context, targets, count):
+def token_blocks(query, keys, values, context, targets):
     pairs = values.shape[0]
     low = lax.broadcasted_iota(jnp.int32, (BLK, BLK), 1) < HEAD_DIM
     real = lax.broadcasted_iota(jnp.int32, (PAD, 2 * BLK), 0) < NB
-    seen = count * BLK
-    chains = [(place, block, first, p) for p in range(pairs) for place, block, first in targets]
+    chains = [
+        (place, block, pl.multiple_of(first * BLK, BLK), count * BLK, p)
+        for p in range(pairs)
+        for place, block, first, count in targets
+    ]
     scores = []
-    for place, block, first, p in chains:
+    for place, block, start, seen, p in chains:
         cols = slice(p * BLK, (p + 1) * BLK)
-        start = pl.multiple_of(first * BLK, BLK)
         q = query[pl.ds(pl.multiple_of(block * BLK, BLK), BLK), cols]
         none = jnp.zeros_like(q)
         both = jnp.concatenate([jnp.where(low, q, none), jnp.where(low, none, q)], axis=0)
@@ -175,11 +179,10 @@
             jnp.concatenate([jnp.exp(s - top).astype(BF16), jnp.exp(se - top).astype(BF16)], axis=0)
         )
     sums = []
-    for (place, block, first, p), part in zip(chains, parts):
-        start = pl.multiple_of(first * BLK, BLK)
+    for (place, block, start, seen, p), part in zip(chains, parts):
         v = jnp.concatenate([values[p, :, pl.ds(start, seen)], values[p, :, CLIP_ROWS:END]], axis=1)
         sums.append(jnp.dot(v, part, preferred_element_type=F32))
-    for (place, block, first, p), o in zip(chains, sums):
+    for (place, block, start, seen, p), o in zip(chains, sums):
         total = o[BLK : BLK + 1]
         o = jnp.concatenate(
             [o[:HEAD_DIM, :BLK] / total[:, :BLK], o[HEAD_DIM:BLK, BLK:] / total[:, BLK:]], axis=0
@@ -199,29 +202,21 @@
 
 def visit_blocks(info, places, query, keys, values, context):
     sights = [sight(info, place) for place in places]
-    if len(places) == 2:
-        alike = sights[0][2] == sights[1][2]
-        for count in range(1, SLOT_DEV):
-
-            @pl.when(alike & (sights[0][2] == count))
-            def _():
-                targets = [(i, block, first) for i, (block, first, _) in enumerate(sights)]
-                token_blocks(query, keys, values, context, targets, count)
-
-    else:
-        alike = False
-
-    def visit(i, carry):
-        block, first, seen = sight(info, places[0] + i * (places[-1] - places[0]))
-        for count in range(1, SLOT_DEV):
-
-            @pl.when(jnp.logical_not(alike) & (seen == count))
-            def _():
-                token_blocks(query, keys, values, context, [(i, block, first)], count)
-
-        return carry
-
-    lax.fori_loop(0, len(places), visit, 0)
+    for counts in itertools.product(range(SLOT_DEV), repeat=len(places)):
+        targets = [
+            (i, block, first, count)
+            for i, ((block, first, _), count) in enumerate(zip(sights, counts))
+            if count
+        ]
+        if not targets:
+            continue
+        match = sights[0][2] == counts[0]
+        for (_, _, seen), count in zip(sights[1:], counts[1:]):
+            match = match & (seen == count)
+
+        @pl.when(match)
+        def _():
+            token_blocks(query, keys, values, context, targets)
 
 
 def attend_kernel(

time: 41.2 us -> 41.7 us (1.012)
  Pallas kernels: 15.4 us -> 17.3 us
  starting transfers between devices: 9.29 us -> 7.98 us
    ppermute x6, starting transfers between devices: 8.92 us -> 7.61 us  [partner(): lax.ppermute(x, 'clip', [(i, i ^ step) for i in range(lax.axis_size('clip...]
    pallas_call x2, Pallas kernels: 2.57 us -> 3.84 us  [part(): pl.pallas_call(kernel, name=name, out_shape=spec((rows, width)), in_specs...]
    pallas_call x1, Pallas kernels: 2.93 us -> 3.57 us  [attend(): pl.pallas_call(attend_kernel, name='attend', out_shape=(block, block, spe...]
  transfers between devices with their start and end apart: 7 -> 7, of which waited for: 0 -> 0; matrix products, arithmetic and copies ran while one was open for 0% -> 0% of each run, Pallas kernels for 19% -> 24%
where the time goes in v5:
time: 41.7 us; the launch traced here: 41.5 us
  Pallas kernels  17.3 us (41%)
  blocking collectives  15.3 us (37%)
  starting transfers between devices  7.98 us (19%)
  between operations  0.78 us (2%)
    ppermute x6, starting transfers between devices, partner(): lax.ppermute(x, 'clip', [(i, i ^ step) for i in range(lax.axis_size('clip...  7.61 us
    pallas_call x1, Pallas kernels, feed(): pl.pallas_call(feed_kernel, name='feed', out_shape=(spec((ROWS, width), F...  5.53 us
    all_gather x2, blocking collectives, body(): lax.all_gather(jnp.concatenate([far, near, across], axis=0), 'mp', axis=0)  5.23 us
    all_gather x1, blocking collectives, body(): stored_all = lax.all_gather(stored, 'mp', axis=0)  4.9 us
    pallas_call x2, Pallas kernels, part(): pl.pallas_call(kernel, name=name, out_shape=spec((rows, width)), in_specs...  3.84 us
    pallas_call x1, Pallas kernels, attend(): pl.pallas_call(attend_kernel, name='attend', out_shape=(block, block, spe...  3.57 us
    all_gather x1, blocking collectives, body(): own_all = lax.all_gather(own, 'mp', axis=0)  2.8 us
    pallas_call x1, Pallas kernels, ready(): pl.pallas_call(ready_kernel, name='ready', out_shape=(spec(w_qkv.shape),...  2.45 us
  transfers between devices with their start and end apart: 7, of which 0 were waited for; matrix products, arithmetic and copies ran while one was open for 0% of the time, Pallas kernels for 24%

profile of v5, /device:TPU:1, one launch (start us, length us, event | category | flops | bytes accessed | tf_op | source)
XLA Modules:
  0.0 41.5 jit_solution(6577761297185988856)
XLA Ops:
  0.6 1.1 %pack.1 = (bf16[128,512]{1,0:T(8,128)(2,1)S(1)}, bf16[128,512]{1,0:T(8,128)(2,1)S(1)}, bf16[128,512]{1,0:T(8,128)(2,1)S(1)}, bf16[400,512]{1,0:T(8,128)(2,1)S(1)}) custom-call(s32[3,128]{1,0:T(4,128)} %bitcast.14, bf16[3,128,512]{2,1,0:T(8,128)(2,1)} %tokens.1, bf16[1,4,512]{2,1,0:T(4,128)(2,1)} %extra.1), custom_call_target="tpu_custom_call" | custom-call | tf_op jit(solution)/shard_map/pack/pallas_call | solution.py:539
  1.7 3.7 %collective-permute-start = (bf16[128,512]{1,0:T(8,128)(2,1)S(1)}, bf16[128,512]{1,0:T(8,128)(2,1)S(1)}, u32[]{:S(2)}, u32[]{:S(2)}) collective-permute-start(bf16[128,512]{1,0:T(8,128)(2,1)S(1)} %get-tuple-element.27), channel_id=1, source_target_pairs={{0,4},{2,6},{4,0},{6,2},{8,12},{10,14},{12,8},{14,10},{16,20},{18,... | collective-permute-start | bytes 393224 | tf_op jit(solution)/shard_map/ppermute | solution.py:35
  5.4 0.3 collective-permute-start.1
  5.7 0.6 %collective-permute-start.2 = (bf16[128,512]{1,0:T(8,128)(2,1)S(1)}, bf16[128,512]{1,0:T(8,128)(2,1)S(1)}, u32[]{:S(2)}, u32[]{:S(2)}) collective-permute-start(bf16[128,512]{1,0:T(8,128)(2,1)S(1)} %get-tuple-element.29), channel_id=1, source_target_pairs={{0,6},{2,4},{4,2},{6,0},{8,14},{10,12},{12,10},{14,8},{16,22},{18,... | collective-permute-start | bytes 393224 | tf_op jit(solution)/shard_map/ppermute | solution.py:35
  6.3 4.9 %all-gather = bf16[800,512]{1,0:T(8,128)(2,1)S(1)} all-gather(bf16[400,512]{1,0:T(8,128)(2,1)S(1)} %get-tuple-element.23), channel_id=2, replica_groups=mesh['clip'=128,'mp'=2] {'mp'}, dimensions={0}, use_global_device_ids=true | all-gather | bytes 1228800 | tf_op jit(solution)/shard_map/all_gather | solution.py:556
  11.2 0.4 collective-permute-start.6
  11.5 2.4 %ready.1 = (bf16[3,1024,512]{2,1,0:T(8,128)(2,1)S(1)}, bf16[144,512]{1,0:T(8,128)(2,1)S(1)}, bf16[144,512]{1,0:T(8,128)(2,1)S(1)}, bf16[4,128,144]{2,1,0:T(8,128...) custom-call(s32[3,128]{1,0:T(4,128)} %bitcast.15, s32[128]{0:T(128)} %all_lengths.1, s32[128]{0:T(128)} %all_videos.1, ...), custom_call_target="tpu_custom_call" | custom-call | flops 450000000 | bytes 4000000 | tf_op jit(solution)/shard_map/ready/pallas_call | solution.py:425
  14.0 0.0 collective-permute-done
  14.0 0.0 collective-permute-done.1
  14.0 0.0 collective-permute-done.2
  14.1 2.4 %all-gather.1 = bf16[768,512]{1,0:T(8,128)(2,1)S(1)} all-gather(bf16[384,512]{1,0:T(8,128)(2,1)S(1)} %pad_maximum_fusion), channel_id=3, replica_groups=mesh['clip'=128,'mp'=2] {'mp'}, dimensions={0}, use_global_device_ids=true | all-gather | bytes 1179648 | tf_op jit(solution)/shard_map/all_gather | solution.py:562
  16.4 0.0 copy-start.2
  16.4 3.6 %attend.1 = (bf16[128,512]{1,0:T(8,128)(2,1)S(1)}, bf16[128,512]{1,0:T(8,128)(2,1)S(1)}, bf16[768,512]{1,0:T(8,128)(2,1)S(1)}, bf16[768,512]{1,0:T(8,128)(2,1)S(1)}, bf16[4,144,768]{2,1,0:T(8,128)(2,1)S(1)}) custom-call(s32[1,8]{1,0:T(1,128)S(1)} %get-tuple-element.25.facts, f32[1,1024]{1,0:T(1,128)S(1)} %get-tuple-element.26.gain, ...), custom_call_target="tpu_custom_call" | custom-call | flops 1800000000 | bytes 6000000 | tf_op jit(solution)/shard_map/attend/pallas_call | solution.py:457
  20.0 0.0 copy-start
  20.0 0.0 copy-start.1
  20.0 0.0 copy-start.3
  20.0 0.0 copy-start.4
  20.1 0.8 %collective-permute-start.3 = (bf16[128,512]{1,0:T(8,128)(2,1)S(1)}, bf16[128,512]{1,0:T(8,128)(2,1)S(1)}, u32[]{:S(2)}, u32[]{:S(2)}) collective-permute-start(bf16[128,512]{1,0:T(8,128)(2,1)S(1)} %get-tuple-element.37), channel_id=1, source_target_pairs={{0,4},{2,6},{4,0},{6,2},{8,12},{10,14},{12,8},{14,10},{16,20},{18,... | collective-permute-start | bytes 393224 | tf_op jit(solution)/shard_map/ppermute | solution.py:35
  20.9 1.5 %near.1 = bf16[128,512]{1,0:T(8,128)(2,1)S(1)} custom-call(bf16[768,512]{1,0:T(8,128)(2,1)S(1)} %get-tuple-element.34.query, bf16[768,512]{1,0:T(8,128)(2,1)S(1)} %get-tuple-element.35.keys, bf16[4,144,768]{2,1,0:T(8,128)(2,1)S(1)} %get-tuple-element.36.values, s32[1,8]{1,0:T(1,128)S(1)} %get-tuple-element.25.facts), custom_call_target="tpu_custom_call" | custom-call | flops 400000000 | bytes 3000000 | tf_op jit(solution)/shard_map/near/pallas_call | solution.py:482
  22.4 0.4 collective-permute-start.4
  22.8 1.8 %collective-permute-start.5 = (bf16[128,512]{1,0:T(8,128)(2,1)S(1)}, bf16[128,512]{1,0:T(8,128)(2,1)S(1)}, u32[]{:S(2)}, u32[]{:S(2)}) collective-permute-start(bf16[128,512]{1,0:T(8,128)(2,1)S(1)} %get-tuple-element.40), channel_id=1, source_target_pairs={{0,6},{2,4},{4,2},{6,0},{8,14},{10,12},{12,10},{14,8},{16,22},{18,... | collective-permute-start | bytes 393224 | tf_op jit(solution)/shard_map/ppermute | solution.py:35
  24.7 2.3 %own.1 = bf16[144,512]{1,0:T(8,128)(2,1)S(1)} custom-call(bf16[768,512]{1,0:T(8,128)(2,1)S(1)} %get-tuple-element.34.query, bf16[768,512]{1,0:T(8,128)(2,1)S(1)} %get-tuple-element.35.keys, bf16[4,144,768]{2,1,0:T(8,128)(2,1)S(1)} %get-tuple-element.36.values, s32[1,8]{1,0:T(1,128)S(1)} %get-tuple-element.25.facts), custom_call_target="tpu_custom_call" | custom-call | flops 400000000 | bytes 3000000 | tf_op jit(solution)/shard_map/own/pallas_call | solution.py:482
  27.0 0.0 collective-permute-done.3
  27.0 2.8 %all-gather.2 = bf16[288,512]{1,0:T(8,128)(2,1)S(1)} all-gather(bf16[144,512]{1,0:T(8,128)(2,1)S(1)} %own.1), channel_id=4, replica_groups=mesh['clip'=128,'mp'=2] {'mp'}, dimensions={0}, use_global_device_ids=true | all-gather | bytes 442368 | tf_op jit(solution)/shard_map/all_gather | solution.py:571
  29.8 0.0 collective-permute-done.4
  29.8 0.0 collective-permute-done.5
  29.8 2.9 %all-gather.3 = bf16[768,512]{1,0:T(8,128)(2,1)S(1)} all-gather(bf16[384,512]{1,0:T(8,128)(2,1)S(1)} %pad_maximum_fusion.1), channel_id=5, replica_groups=mesh['clip'=128,'mp'=2] {'mp'}, dimensions={0}, use_global_device_ids=true | all-gather | bytes 1179648 | tf_op jit(solution)/shard_map/all_gather | solution.py:572
  32.7 0.0 collective-permute-done.6.w_out_other
  32.7 0.0 copy-done.2
  32.7 0.0 copy-done
  32.7 0.0 copy-done.1
  32.7 0.0 copy-done.3
  32.7 0.0 copy-done.4
  32.7 5.5 %feed.1 = (f32[400,512]{1,0:T(8,128)S(1)}, bf16[400,512]{1,0:T(8,128)(2,1)S(1)}) custom-call(s32[3,128]{1,0:T(4,128)S(1)} %bitcast.16, bf16[2,400,512]{2,1,0:T(8,128)(2,1)S(1)} %bitcast.9, bf16[2,144,512]{2,1,0:T(8,128)(2,1)S(1)} %bitcast.13, bf16[2,384,512]{2,1,0:T(8,128)(2,1)S(1)} %bitcast.12, bf16[512,1024]{1,0:T(8,128)(2,1)S(1)} %copy-done.3, ...), custom_call_target="tpu_custom_call" | custom-call | flops 4100000000 | bytes 14000000 | tf_op jit(solution)/shard_map/feed/pallas_call | solution.py:502
  38.3 2.4 %all-gather.4 = bf16[800,512]{1,0:T(8,128)(2,1)S(1)} all-gather(bf16[400,512]{1,0:T(8,128)(2,1)S(1)} %get-tuple-element.43), channel_id=6, replica_groups=mesh['clip'=128,'mp'=2] {'mp'}, dimensions={0}, use_global_device_ids=true | all-gather | bytes 1228800 | tf_op jit(solution)/shard_map/all_gather | solution.py:577
  40.7 0.9 %finish.1 = (bf16[3,128,512]{2,1,0:T(8,128)(2,1)}, bf16[1,4,512]{2,1,0:T(4,128)(2,1)}) custom-call(f32[400,512]{1,0:T(8,128)S(1)} %get-tuple-element.42.base, bf16[2,400,512]{2,1,0:T(8,128)(2,1)S(1)} %bitcast.10), custom_call_target="tpu_custom_call" | custom-call | tf_op jit(solution)/shard_map/finish/pallas_call | solution.py:579
  (2 shorter events, 0.1 us)
Async XLA Ops:
  1.7 12.3 %collective-permute-start = (bf16[128,512]{1,0:T(8,128)(2,1)S(1)}, bf16[128,512]{1,0:T(8,128)(2,1)S(1)}, u32[]{:S(2)}, u32[]{:S(2)}) collective-permute-start(bf16[128,512]{1,0:T(8,128)(2,1)S(1)} %get-tuple-element.27), channel_id=1, source_target_pairs={{0,4},{2,6},{4,0},{6,2},{8,12},{10,14},{12,8},{14,10},{16,20},{18,... | collective-permute-start | bytes 393224 | tf_op jit(solution)/shard_map/ppermute | solution.py:35
  5.4 8.6 %collective-permute-start.1 = (bf16[128,512]{1,0:T(8,128)(2,1)S(1)}, bf16[128,512]{1,0:T(8,128)(2,1)S(1)}, u32[]{:S(2)}, u32[]{:S(2)}) collective-permute-start(bf16[128,512]{1,0:T(8,128)(2,1)S(1)} %get-tuple-element.28), channel_id=1, source_target_pairs={{0,2},{2,0},{4,6},{6,4},{8,10},{10,8},{12,14},{14,12},{16,18},{18,... | collective-permute-start | bytes 393224 | tf_op jit(solution)/shard_map/ppermute | solution.py:35
  5.7 8.3 %collective-permute-start.2 = (bf16[128,512]{1,0:T(8,128)(2,1)S(1)}, bf16[128,512]{1,0:T(8,128)(2,1)S(1)}, u32[]{:S(2)}, u32[]{:S(2)}) collective-permute-start(bf16[128,512]{1,0:T(8,128)(2,1)S(1)} %get-tuple-element.29), channel_id=1, source_target_pairs={{0,6},{2,4},{4,2},{6,0},{8,14},{10,12},{12,10},{14,8},{16,22},{18,... | collective-permute-start | bytes 393224 | tf_op jit(solution)/shard_map/ppermute | solution.py:35
  11.2 21.5 %collective-permute-start.6 = (bf16[512,1024]{1,0:T(8,128)(2,1)}, bf16[512,1024]{1,0:T(8,128)(2,1)S(1)}, u32[]{:S(2)}, u32[]{:S(2)}) collective-permute-start(bf16[512,1024]{1,0:T(8,128)(2,1)} %w_out.1), channel_id=1, source_target_pairs={{0,1},{1,0},{2,3},{3,2},{4,5},{5,4},{6,7},{7,6},{8,9},{9,8},{10,11... | collective-permute-start | bytes 3145736 | tf_op jit(solution)/shard_map/ppermute | solution.py:558
  16.4 16.3 %copy-start.2 = (bf16[2048,1024]{1,0:T(8,128)(2,1)S(1)}, bf16[2048,1024]{1,0:T(8,128)(2,1)}, u32[]{:S(2)}) copy-start(bf16[2048,1024]{1,0:T(8,128)(2,1)} %w_down.1) | copy-start | bytes 12582916
  20.0 12.7 %copy-start = (s32[128,3]{0,1:T(4,128)S(1)}, s32[128,3]{0,1:T(4,128)}, u32[]{:S(2)}) copy-start(s32[128,3]{0,1:T(4,128)} %param.15) | copy-start | bytes 4612
  20.0 12.7 %copy-start.1 = (bf16[1024,2048]{1,0:T(8,128)(2,1)S(1)}, bf16[1024,2048]{1,0:T(8,128)(2,1)}, u32[]{:S(2)}) copy-start(bf16[1024,2048]{1,0:T(8,128)(2,1)} %w_up.1) | copy-start | bytes 12582916
  20.0 12.7 %copy-start.3 = (bf16[512,1024]{1,0:T(8,128)(2,1)S(1)}, bf16[512,1024]{1,0:T(8,128)(2,1)}, u32[]{:S(2)}) copy-start(bf16[512,1024]{1,0:T(8,128)(2,1)} %w_out.1) | copy-start | bytes 3145732
  20.0 12.7 %copy-start.4 = (f32[1024]{0:T(1024)S(1)}, f32[1024]{0:T(1024)}, u32[]{:S(2)}) copy-start(f32[1024]{0:T(1024)} %param.19) | copy-start | bytes 12292
  20.1 6.9 %collective-permute-start.3 = (bf16[128,512]{1,0:T(8,128)(2,1)S(1)}, bf16[128,512]{1,0:T(8,128)(2,1)S(1)}, u32[]{:S(2)}, u32[]{:S(2)}) collective-permute-start(bf16[128,512]{1,0:T(8,128)(2,1)S(1)} %get-tuple-element.37), channel_id=1, source_target_pairs={{0,4},{2,6},{4,0},{6,2},{8,12},{10,14},{12,8},{14,10},{16,20},{18,... | collective-permute-start | bytes 393224 | tf_op jit(solution)/shard_map/ppermute | solution.py:35
  22.4 7.4 %collective-permute-start.4 = (bf16[128,512]{1,0:T(8,128)(2,1)S(1)}, bf16[128,512]{1,0:T(8,128)(2,1)S(1)}, u32[]{:S(2)}, u32[]{:S(2)}) collective-permute-start(bf16[128,512]{1,0:T(8,128)(2,1)S(1)} %near.1), channel_id=1, source_target_pairs={{0,2},{2,0},{4,6},{6,4},{8,10},{10,8},{12,14},{14,12},{16,18},{18,... | collective-permute-start | bytes 393224 | tf_op jit(solution)/shard_map/ppermute | solution.py:35
  22.8 7.0 %collective-permute-start.5 = (bf16[128,512]{1,0:T(8,128)(2,1)S(1)}, bf16[128,512]{1,0:T(8,128)(2,1)S(1)}, u32[]{:S(2)}, u32[]{:S(2)}) collective-permute-start(bf16[128,512]{1,0:T(8,128)(2,1)S(1)} %get-tuple-element.40), channel_id=1, source_target_pairs={{0,6},{2,4},{4,2},{6,0},{8,14},{10,12},{12,10},{14,8},{16,22},{18,... | collective-permute-start | bytes 393224 | tf_op jit(solution)/shard_map/ppermute | solution.py:35

commit v6 on v3

--- a/solution.py
+++ b/solution.py
@@ -16,6 +16,7 @@
 ROWS = STORED + PAD
 CLIP_ROWS = SLOT_DEV * BLK
 STEPS = (2, 1, 3)
+BACK = (2, 3, 1)
 BF16 = jnp.bfloat16
 F32 = jnp.float32
 
@@ -371,7 +372,7 @@
     for s in range(STORE_DEV):
         entry = store_map[s, member]
         step = jnp.where(entry >= 0, (entry // SLOT_DEV) ^ member, -1)
-        at = jnp.where(step == STEPS[0], 0, jnp.where(step == STEPS[1], 1, 2))
+        at = jnp.where(step == BACK[0], 0, jnp.where(step == BACK[1], 1, 2))
         at = pl.multiple_of(at * BLK, BLK)
         rows = slice(s * BLK, (s + 1) * BLK)
         mine = jnp.full((BLK, half), step, jnp.int32) == 0
@@ -568,13 +569,14 @@
 
     far, across, query, keys, values = attend(facts, gain, arrived, weights, own_qkv)
     far = partner(far, 2)
+    near = part(near_kernel, "near", BLK, query, keys, values, facts)
+    across, near = lax.optimization_barrier((across, near))
     across = partner(across, 3)
-    near = part(near_kernel, "near", BLK, query, keys, values, facts)
     near = partner(near, 1)
     own = part(own_kernel, "own", BLK + PAD, query, keys, values, facts)
     own, far = lax.optimization_barrier((own, far))
     own_all = lax.all_gather(own, "mp", axis=0)
-    arrived = lax.all_gather(jnp.concatenate([far, near, across], axis=0), "mp", axis=0)
+    arrived = lax.all_gather(jnp.concatenate([far, across, near], axis=0), "mp", axis=0)
 
     base, send = feed(
         slots, stored_all, own_all, arrived, w_out, w_out_other, gain2, w_up, w_down

time: 41.2 us -> 41.3 us (level)
  Pallas kernels: 15.4 us -> 17.6 us
  starting transfers between devices: 9.29 us -> 7.55 us
  blocking collectives: 15.6 us -> 15 us
    all_gather x2 -> x1, blocking collectives: 5.54 us -> 2.37 us  [body(): lax.all_gather(jnp.concatenate([far, near, across], axis=0), 'mp', axis=0)]
    all_gather x0 -> x1, blocking collectives: none -> 2.68 us  [body(): lax.all_gather(jnp.concatenate([far, across, near], axis=0), 'mp', axis=0)]
    ppermute x6, starting transfers between devices: 8.92 us -> 7.18 us  [partner(): lax.ppermute(x, 'clip', [(i, i ^ step) for i in range(lax.axis_size('clip...]
    pallas_call x2, Pallas kernels: 2.57 us -> 3.84 us  [part(): pl.pallas_call(kernel, name=name, out_shape=spec((rows, width)), in_specs...]
    pallas_call x1, Pallas kernels: 2.93 us -> 3.83 us  [attend(): pl.pallas_call(attend_kernel, name='attend', out_shape=(block, block, spe...]
  transfers between devices with their start and end apart: 7 -> 7, of which waited for: 0 -> 1; matrix products, arithmetic and copies ran while one was open for 0% -> 0% of each run, Pallas kernels for 19% -> 24%
where the time goes in v6:
time: 41.3 us; the launch traced here: 41.5 us
  Pallas kernels  17.6 us (43%)
  blocking collectives  15 us (36%)
  starting transfers between devices  7.55 us (18%)
  between operations  0.79 us (2%)
    ppermute x6, starting transfers between devices, partner(): lax.ppermute(x, 'clip', [(i, i ^ step) for i in range(lax.axis_size('clip...  7.18 us
    pallas_call x1, Pallas kernels, feed(): pl.pallas_call(feed_kernel, name='feed', out_shape=(spec((ROWS, width), F...  5.53 us
    all_gather x1, blocking collectives, body(): stored_all = lax.all_gather(stored, 'mp', axis=0)  4.9 us
    pallas_call x2, Pallas kernels, part(): pl.pallas_call(kernel, name=name, out_shape=spec((rows, width)), in_specs...  3.84 us
    pallas_call x1, Pallas kernels, attend(): pl.pallas_call(attend_kernel, name='attend', out_shape=(block, block, spe...  3.83 us
    all_gather x1, blocking collectives, body(): own_all = lax.all_gather(own, 'mp', axis=0)  2.7 us
    all_gather x1, blocking collectives, body(): lax.all_gather(jnp.concatenate([far, across, near], axis=0), 'mp', axis=0)  2.68 us
    pallas_call x1, Pallas kernels, ready(): pl.pallas_call(ready_kernel, name='ready', out_shape=(spec(w_qkv.shape),...  2.45 us
  transfers between devices with their start and end apart: 7, of which 1 were waited for; matrix products, arithmetic and copies ran while one was open for 0% of the time, Pallas kernels for 24%

profile of v6, /device:TPU:1, one launch (start us, length us, event | category | flops | bytes accessed | tf_op | source)
XLA Modules:
  0.0 41.5 jit_solution(9552201724855893284)
XLA Ops:
  0.6 1.1 %pack.1 = (bf16[128,512]{1,0:T(8,128)(2,1)S(1)}, bf16[128,512]{1,0:T(8,128)(2,1)S(1)}, bf16[128,512]{1,0:T(8,128)(2,1)S(1)}, bf16[400,512]{1,0:T(8,128)(2,1)S(1)}) custom-call(s32[3,128]{1,0:T(4,128)} %bitcast.14, bf16[3,128,512]{2,1,0:T(8,128)(2,1)} %tokens.1, bf16[1,4,512]{2,1,0:T(4,128)(2,1)} %extra.1), custom_call_target="tpu_custom_call" | custom-call | tf_op jit(solution)/shard_map/pack/pallas_call | solution.py:545
  1.7 3.7 %collective-permute-start = (bf16[128,512]{1,0:T(8,128)(2,1)S(1)}, bf16[128,512]{1,0:T(8,128)(2,1)S(1)}, u32[]{:S(2)}, u32[]{:S(2)}) collective-permute-start(bf16[128,512]{1,0:T(8,128)(2,1)S(1)} %get-tuple-element.29), channel_id=1, source_target_pairs={{0,4},{2,6},{4,0},{6,2},{8,12},{10,14},{12,8},{14,10},{16,20},{18,... | collective-permute-start | bytes 393224 | tf_op jit(solution)/shard_map/ppermute | solution.py:34
  5.4 0.3 collective-permute-start.1
  5.7 0.6 %collective-permute-start.2 = (bf16[128,512]{1,0:T(8,128)(2,1)S(1)}, bf16[128,512]{1,0:T(8,128)(2,1)S(1)}, u32[]{:S(2)}, u32[]{:S(2)}) collective-permute-start(bf16[128,512]{1,0:T(8,128)(2,1)S(1)} %get-tuple-element.31), channel_id=1, source_target_pairs={{0,6},{2,4},{4,2},{6,0},{8,14},{10,12},{12,10},{14,8},{16,22},{18,... | collective-permute-start | bytes 393224 | tf_op jit(solution)/shard_map/ppermute | solution.py:34
  6.3 4.9 %all-gather = bf16[800,512]{1,0:T(8,128)(2,1)S(1)} all-gather(bf16[400,512]{1,0:T(8,128)(2,1)S(1)} %get-tuple-element.25), channel_id=2, replica_groups=mesh['clip'=128,'mp'=2] {'mp'}, dimensions={0}, use_global_device_ids=true | all-gather | bytes 1228800 | tf_op jit(solution)/shard_map/all_gather | solution.py:562
  11.2 0.4 collective-permute-start.6
  11.5 2.4 %ready.1 = (bf16[3,1024,512]{2,1,0:T(8,128)(2,1)S(1)}, bf16[144,512]{1,0:T(8,128)(2,1)S(1)}, bf16[144,512]{1,0:T(8,128)(2,1)S(1)}, bf16[4,128,144]{2,1,0:T(8,128...) custom-call(s32[3,128]{1,0:T(4,128)} %bitcast.15, s32[128]{0:T(128)} %all_lengths.1, s32[128]{0:T(128)} %all_videos.1, ...), custom_call_target="tpu_custom_call" | custom-call | flops 450000000 | bytes 4000000 | tf_op jit(solution)/shard_map/ready/pallas_call | solution.py:431
  14.0 0.0 collective-permute-done
  14.0 0.0 collective-permute-done.1
  14.0 0.0 collective-permute-done.2
  14.1 2.4 %all-gather.1 = bf16[768,512]{1,0:T(8,128)(2,1)S(1)} all-gather(bf16[384,512]{1,0:T(8,128)(2,1)S(1)} %pad_maximum_fusion), channel_id=3, replica_groups=mesh['clip'=128,'mp'=2] {'mp'}, dimensions={0}, use_global_device_ids=true | all-gather | bytes 1179648 | tf_op jit(solution)/shard_map/all_gather | solution.py:568
  16.4 0.0 copy-start.2
  16.4 3.8 %attend.1 = (bf16[128,512]{1,0:T(8,128)(2,1)S(1)}, bf16[128,512]{1,0:T(8,128)(2,1)S(1)}, bf16[768,512]{1,0:T(8,128)(2,1)S(1)}, bf16[768,512]{1,0:T(8,128)(2,1)S(1)}, bf16[4,144,768]{2,1,0:T(8,128)(2,1)S(1)}) custom-call(s32[1,8]{1,0:T(1,128)S(1)} %get-tuple-element.27.facts, f32[1,1024]{1,0:T(1,128)S(1)} %get-tuple-element.28.gain, ...), custom_call_target="tpu_custom_call" | custom-call | flops 1800000000 | bytes 6000000 | tf_op jit(solution)/shard_map/attend/pallas_call | solution.py:463
  20.3 0.0 copy-start
  20.3 0.0 copy-start.1
  20.3 0.0 copy-start.3
  20.3 0.0 copy-start.4
  20.3 0.6 %collective-permute-start.3 = (bf16[128,512]{1,0:T(8,128)(2,1)S(1)}, bf16[128,512]{1,0:T(8,128)(2,1)S(1)}, u32[]{:S(2)}, u32[]{:S(2)}) collective-permute-start(bf16[128,512]{1,0:T(8,128)(2,1)S(1)} %get-tuple-element.39), channel_id=1, source_target_pairs={{0,4},{2,6},{4,0},{6,2},{8,12},{10,14},{12,8},{14,10},{16,20},{18,... | collective-permute-start | bytes 393224 | tf_op jit(solution)/shard_map/ppermute | solution.py:34
  20.9 1.5 %near.1 = bf16[128,512]{1,0:T(8,128)(2,1)S(1)} custom-call(bf16[768,512]{1,0:T(8,128)(2,1)S(1)} %get-tuple-element.36.query, bf16[768,512]{1,0:T(8,128)(2,1)S(1)} %get-tuple-element.37.keys, bf16[4,144,768]{2,1,0:T(8,128)(2,1)S(1)} %get-tuple-element.38.values, s32[1,8]{1,0:T(1,128)S(1)} %get-tuple-element.27.facts), custom_call_target="tpu_custom_call" | custom-call | flops 400000000 | bytes 3000000 | tf_op jit(solution)/shard_map/near/pallas_call | solution.py:488
  22.4 0.3 collective-permute-start.4
  22.7 1.8 %collective-permute-start.5 = (bf16[128,512]{1,0:T(8,128)(2,1)S(1)}, bf16[128,512]{1,0:T(8,128)(2,1)S(1)}, u32[]{:S(2)}, u32[]{:S(2)}) collective-permute-start(bf16[128,512]{1,0:T(8,128)(2,1)S(1)} %near.1), channel_id=1, source_target_pairs={{0,2},{2,0},{4,6},{6,4},{8,10},{10,8},{12,14},{14,12},{16,18},{18,... | collective-permute-start | bytes 393224 | tf_op jit(solution)/shard_map/ppermute | solution.py:34
  24.5 2.3 %own.1 = bf16[144,512]{1,0:T(8,128)(2,1)S(1)} custom-call(bf16[768,512]{1,0:T(8,128)(2,1)S(1)} %get-tuple-element.36.query, bf16[768,512]{1,0:T(8,128)(2,1)S(1)} %get-tuple-element.37.keys, bf16[4,144,768]{2,1,0:T(8,128)(2,1)S(1)} %get-tuple-element.38.values, s32[1,8]{1,0:T(1,128)S(1)} %get-tuple-element.27.facts), custom_call_target="tpu_custom_call" | custom-call | flops 400000000 | bytes 3000000 | tf_op jit(solution)/shard_map/own/pallas_call | solution.py:488
  26.8 0.0 collective-permute-done.3
  26.8 2.7 %all-gather.2 = bf16[288,512]{1,0:T(8,128)(2,1)S(1)} all-gather(bf16[144,512]{1,0:T(8,128)(2,1)S(1)} %own.1), channel_id=4, replica_groups=mesh['clip'=128,'mp'=2] {'mp'}, dimensions={0}, use_global_device_ids=true | all-gather | bytes 442368 | tf_op jit(solution)/shard_map/all_gather | solution.py:578
  29.5 0.4 collective-permute-done.4
  29.9 0.0 collective-permute-done.5
  30.0 2.7 %all-gather.3 = bf16[768,512]{1,0:T(8,128)(2,1)S(1)} all-gather(bf16[384,512]{1,0:T(8,128)(2,1)S(1)} %pad_maximum_fusion.1), channel_id=5, replica_groups=mesh['clip'=128,'mp'=2] {'mp'}, dimensions={0}, use_global_device_ids=true | all-gather | bytes 1179648 | tf_op jit(solution)/shard_map/all_gather | solution.py:579
  32.7 0.0 collective-permute-done.6.w_out_other
  32.7 0.0 copy-done.2
  32.7 0.0 copy-done
  32.7 0.0 copy-done.1
  32.7 0.0 copy-done.3
  32.7 0.0 copy-done.4
  32.7 5.5 %feed.1 = (f32[400,512]{1,0:T(8,128)S(1)}, bf16[400,512]{1,0:T(8,128)(2,1)S(1)}) custom-call(s32[3,128]{1,0:T(4,128)S(1)} %bitcast.16, bf16[2,400,512]{2,1,0:T(8,128)(2,1)S(1)} %bitcast.9, bf16[2,144,512]{2,1,0:T(8,128)(2,1)S(1)} %bitcast.13, bf16[2,384,512]{2,1,0:T(8,128)(2,1)S(1)} %bitcast.12, bf16[512,1024]{1,0:T(8,128)(2,1)S(1)} %copy-done.3, ...), custom_call_target="tpu_custom_call" | custom-call | flops 4100000000 | bytes 14000000 | tf_op jit(solution)/shard_map/feed/pallas_call | solution.py:508
  38.2 2.4 %all-gather.4 = bf16[800,512]{1,0:T(8,128)(2,1)S(1)} all-gather(bf16[400,512]{1,0:T(8,128)(2,1)S(1)} %get-tuple-element.47), channel_id=6, replica_groups=mesh['clip'=128,'mp'=2] {'mp'}, dimensions={0}, use_global_device_ids=true | all-gather | bytes 1228800 | tf_op jit(solution)/shard_map/all_gather | solution.py:584
  40.6 0.9 %finish.1 = (bf16[3,128,512]{2,1,0:T(8,128)(2,1)}, bf16[1,4,512]{2,1,0:T(4,128)(2,1)}) custom-call(f32[400,512]{1,0:T(8,128)S(1)} %get-tuple-element.46.base, bf16[2,400,512]{2,1,0:T(8,128)(2,1)S(1)} %bitcast.10), custom_call_target="tpu_custom_call" | custom-call | tf_op jit(solution)/shard_map/finish/pallas_call | solution.py:586
  (2 shorter events, 0.1 us)
Async XLA Ops:
  1.7 12.3 %collective-permute-start = (bf16[128,512]{1,0:T(8,128)(2,1)S(1)}, bf16[128,512]{1,0:T(8,128)(2,1)S(1)}, u32[]{:S(2)}, u32[]{:S(2)}) collective-permute-start(bf16[128,512]{1,0:T(8,128)(2,1)S(1)} %get-tuple-element.29), channel_id=1, source_target_pairs={{0,4},{2,6},{4,0},{6,2},{8,12},{10,14},{12,8},{14,10},{16,20},{18,... | collective-permute-start | bytes 393224 | tf_op jit(solution)/shard_map/ppermute | solution.py:34
  5.4 8.6 %collective-permute-start.1 = (bf16[128,512]{1,0:T(8,128)(2,1)S(1)}, bf16[128,512]{1,0:T(8,128)(2,1)S(1)}, u32[]{:S(2)}, u32[]{:S(2)}) collective-permute-start(bf16[128,512]{1,0:T(8,128)(2,1)S(1)} %get-tuple-element.30), channel_id=1, source_target_pairs={{0,2},{2,0},{4,6},{6,4},{8,10},{10,8},{12,14},{14,12},{16,18},{18,... | collective-permute-start | bytes 393224 | tf_op jit(solution)/shard_map/ppermute | solution.py:34
  5.7 8.3 %collective-permute-start.2 = (bf16[128,512]{1,0:T(8,128)(2,1)S(1)}, bf16[128,512]{1,0:T(8,128)(2,1)S(1)}, u32[]{:S(2)}, u32[]{:S(2)}) collective-permute-start(bf16[128,512]{1,0:T(8,128)(2,1)S(1)} %get-tuple-element.31), channel_id=1, source_target_pairs={{0,6},{2,4},{4,2},{6,0},{8,14},{10,12},{12,10},{14,8},{16,22},{18,... | collective-permute-start | bytes 393224 | tf_op jit(solution)/shard_map/ppermute | solution.py:34
  11.2 21.5 %collective-permute-start.6 = (bf16[512,1024]{1,0:T(8,128)(2,1)}, bf16[512,1024]{1,0:T(8,128)(2,1)S(1)}, u32[]{:S(2)}, u32[]{:S(2)}) collective-permute-start(bf16[512,1024]{1,0:T(8,128)(2,1)} %w_out.1), channel_id=1, source_target_pairs={{0,1},{1,0},{2,3},{3,2},{4,5},{5,4},{6,7},{7,6},{8,9},{9,8},{10,11... | collective-permute-start | bytes 3145736 | tf_op jit(solution)/shard_map/ppermute | solution.py:564
  16.4 16.2 %copy-start.2 = (bf16[2048,1024]{1,0:T(8,128)(2,1)S(1)}, bf16[2048,1024]{1,0:T(8,128)(2,1)}, u32[]{:S(2)}) copy-start(bf16[2048,1024]{1,0:T(8,128)(2,1)} %w_down.1) | copy-start | bytes 12582916
  20.3 12.4 %copy-start = (s32[128,3]{0,1:T(4,128)S(1)}, s32[128,3]{0,1:T(4,128)}, u32[]{:S(2)}) copy-start(s32[128,3]{0,1:T(4,128)} %param.15) | copy-start | bytes 4612
  20.3 12.4 %copy-start.1 = (bf16[1024,2048]{1,0:T(8,128)(2,1)S(1)}, bf16[1024,2048]{1,0:T(8,128)(2,1)}, u32[]{:S(2)}) copy-start(bf16[1024,2048]{1,0:T(8,128)(2,1)} %w_up.1) | copy-start | bytes 12582916
  20.3 12.4 %copy-start.3 = (bf16[512,1024]{1,0:T(8,128)(2,1)S(1)}, bf16[512,1024]{1,0:T(8,128)(2,1)}, u32[]{:S(2)}) copy-start(bf16[512,1024]{1,0:T(8,128)(2,1)} %w_out.1) | copy-start | bytes 3145732
  20.3 12.4 %copy-start.4 = (f32[1024]{0:T(1024)S(1)}, f32[1024]{0:T(1024)}, u32[]{:S(2)}) copy-start(f32[1024]{0:T(1024)} %param.19) | copy-start | bytes 12292
  20.3 6.5 %collective-permute-start.3 = (bf16[128,512]{1,0:T(8,128)(2,1)S(1)}, bf16[128,512]{1,0:T(8,128)(2,1)S(1)}, u32[]{:S(2)}, u32[]{:S(2)}) collective-permute-start(bf16[128,512]{1,0:T(8,128)(2,1)S(1)} %get-tuple-element.39), channel_id=1, source_target_pairs={{0,4},{2,6},{4,0},{6,2},{8,12},{10,14},{12,8},{14,10},{16,20},{18,... | collective-permute-start | bytes 393224 | tf_op jit(solution)/shard_map/ppermute | solution.py:34
  22.4 7.5 %collective-permute-start.4 = (bf16[128,512]{1,0:T(8,128)(2,1)S(1)}, bf16[128,512]{1,0:T(8,128)(2,1)S(1)}, u32[]{:S(2)}, u32[]{:S(2)}) collective-permute-start(bf16[128,512]{1,0:T(8,128)(2,1)S(1)} %get-tuple-element.43), channel_id=1, source_target_pairs={{0,6},{2,4},{4,2},{6,0},{8,14},{10,12},{12,10},{14,8},{16,22},{18,... | collective-permute-start | bytes 393224 | tf_op jit(solution)/shard_map/ppermute | solution.py:34
  22.7 7.3 %collective-permute-start.5 = (bf16[128,512]{1,0:T(8,128)(2,1)S(1)}, bf16[128,512]{1,0:T(8,128)(2,1)S(1)}, u32[]{:S(2)}, u32[]{:S(2)}) collective-permute-start(bf16[128,512]{1,0:T(8,128)(2,1)S(1)} %near.1), channel_id=1, source_target_pairs={{0,2},{2,0},{4,6},{6,4},{8,10},{10,8},{12,14},{14,12},{16,18},{18,... | collective-permute-start | bytes 393224 | tf_op jit(solution)/shard_map/ppermute | solution.py:34
